TPU v7x, 256 devices: a whole 4x4x8 slice. The times are simulated.
256 devices in a mesh: dp: 64 (over z, y, core), tp: 4 (over x).
Axes of the slice: x: 4, y: 4, z: 8, core: 2. Of those that a mesh axis runs over, the one named last changes fastest.
Arguments:
- attn_partial: bfloat16 [4, 4096, 7168], P('tp', 'dp'), may hold values from -3 to 3
- hidden_in: bfloat16 [4096, 7168], P('dp', 'tp'), may hold values from -6 to 6
- norm_gain: float32 [7168], replicated, may hold values from 0.5 to 1.5
- expert_ids: int32 [4096, 8], P('dp'), may hold values from 0 to 255, all different within a row; in each aligned block of 64 rows (0 to 63, 64 to 127, ...) at most 4 rows name the same one
- route_prob: bfloat16 [4096, 8], P('dp'), may hold values from 0.049804688 to 0.3984375
- w_gate: bfloat16 [64, 7168, 1024], P('dp', None, 'tp'), may hold values from -0.0625 to 0.0625
- w_up: bfloat16 [64, 7168, 1024], P('dp', None, 'tp'), may hold values from -0.0625 to 0.0625
- w_down: bfloat16 [64, 1024, 7168], P('dp', 'tp'), may hold values from -0.1875 to 0.1875
Outputs:
- layer_out: bfloat16 [4096, 7168], P('dp', 'tp')
- amax_input: float32 [64], P('dp')
- amax_hidden: float32 [64], P('dp')
Inputs may be any that keep to these rules, and one draw needn't show every extreme that they name: `expert_ids`: each token names 8 different experts; within each aligned block of 64 tokens no expert is named by more than 4 tokens.
All inputs are finite; a program needn't handle non-finite values.
Results may differ from a plain program's by a relative error of at most 0.0075.
Values may be sent and summed in bfloat16 or wider, within the bound.
A program may use at most 64 MiB of HBM per device.

v0:
```python
import jax
import jax.numpy as jnp
from jax import lax
from jax.sharding import PartitionSpec as P

EXPERT_SLOTS = 4


eps = 1e-06


def route_tables(expert_ids, route_prob, experts, capacity):
    matches = expert_ids[:, :, None] == jnp.arange(experts, dtype=jnp.int32)[None, None, :]
    onehot = jnp.sum(matches.astype(jnp.int32), axis=1)
    weight = jnp.sum(
        jnp.where(matches, route_prob[:, :, None].astype(jnp.float32), jnp.float32(0.0)), axis=1
    )
    before = jnp.cumsum(onehot, axis=0) - onehot
    placing = (onehot.T[:, None, :] == 1) & (
        before.T[:, None, :] == jnp.arange(capacity, dtype=jnp.int32)[None, :, None]
    )
    return (onehot, weight, placing)


def on_device(attn_partial, hidden_in, norm_gain, expert_ids, route_prob, w_gate, w_up, w_down):
    experts = lax.axis_size("dp")
    dp_index = lax.axis_index("dp")
    tp_index = lax.axis_index("tp")
    partial_value = attn_partial[0].astype(jnp.float32)
    token_count = partial_value.shape[0]
    columns = hidden_in.shape[1]
    start_col = tp_index * columns
    own_cols = lax.dynamic_slice_in_dim(partial_value, start_col, columns, 1) + hidden_in.astype(
        jnp.float32
    )
    summand = lax.dynamic_update_slice_in_dim(partial_value, own_cols, start_col, 1)
    residual = lax.psum(summand, "tp")
    mean_sq = jnp.mean(residual * residual, axis=1, keepdims=True)
    normed = (residual * lax.rsqrt(mean_sq + eps) * norm_gain).astype(jnp.bfloat16)
    residual_cols = lax.dynamic_slice_in_dim(residual, start_col, columns, 1)
    onehot, weight, placing = route_tables(expert_ids, route_prob, experts, EXPERT_SLOTS)
    selection_mask = placing.reshape(experts * EXPERT_SLOTS, token_count).astype(jnp.bfloat16)
    outgoing = jnp.dot(selection_mask, normed, preferred_element_type=jnp.float32).astype(
        jnp.bfloat16
    )
    piece_width = outgoing.shape[1]
    incoming = lax.all_to_all(
        outgoing.reshape(experts, EXPERT_SLOTS, piece_width),
        "dp",
        split_axis=0,
        concat_axis=0,
        tiled=True,
    )
    expert_slot_rows = incoming.reshape(experts * EXPERT_SLOTS, piece_width)
    gate_val = jnp.dot(expert_slot_rows, w_gate[0], preferred_element_type=jnp.float32)
    up_val = jnp.dot(expert_slot_rows, w_up[0], preferred_element_type=jnp.float32)
    hidden_act = (jax.nn.silu(gate_val) * up_val).astype(jnp.bfloat16)
    partial_out = jnp.dot(hidden_act, w_down[0], preferred_element_type=jnp.float32)
    combine_matrix = (placing.astype(jnp.float32) * weight.T[:, None, :]).reshape(
        experts * EXPERT_SLOTS, token_count
    )
    expert_cols = lax.psum_scatter(
        partial_out.astype(jnp.bfloat16), "tp", scatter_dimension=1, tiled=True
    ).astype(jnp.float32)
    returned = lax.all_to_all(
        expert_cols.reshape(experts, EXPERT_SLOTS, columns).astype(jnp.bfloat16),
        "dp",
        split_axis=0,
        concat_axis=0,
        tiled=True,
    ).astype(jnp.float32)
    moe_out = jnp.dot(
        combine_matrix.T,
        returned.reshape(experts * EXPERT_SLOTS, columns),
        precision=lax.Precision.HIGHEST,
        preferred_element_type=jnp.float32,
    )
    layer_out = (residual_cols + moe_out).astype(jnp.bfloat16)
    hidden_peak = jnp.max(jnp.abs(hidden_act.astype(jnp.float32)))
    row_peak = jnp.max(jnp.abs(normed.astype(jnp.float32)), axis=1)
    local_entry = jnp.max(onehot.astype(jnp.float32) * row_peak[:, None], axis=0)
    own_slot = jnp.arange(experts, dtype=jnp.int32) == dp_index
    hidden_local = jnp.where(own_slot, hidden_peak, jnp.float32(0.0))
    every_entry, every_hidden = lax.pmax((local_entry, hidden_local), ("dp", "tp"))
    amax_input = lax.dynamic_slice_in_dim(every_entry, dp_index, 1, 0)
    amax_hidden = lax.dynamic_slice_in_dim(every_hidden, dp_index, 1, 0)
    return (layer_out, amax_input, amax_hidden)


def solution(mesh):
    placed = (
        P("tp", "dp", None),
        P("dp", "tp"),
        P(),
        P("dp", None),
        P("dp", None),
        P("dp", None, "tp"),
        P("dp", None, "tp"),
        P("dp", "tp", None),
    )
    return jax.shard_map(
        on_device,
        mesh=mesh,
        in_specs=placed,
        out_specs=(P("dp", "tp"), P("dp"), P("dp")),
        check_vma=False,
    )
```

profile of v0, /device:TPU:1, one launch (start us, length us, event | category | flops | bytes accessed | tf_op | source)
XLA Modules:
  0.0 342.8 jit_solution(10754556767076830818)
XLA Ops:
  7.2 2.8 fusion.21
  10.1 1.1 fusion.14
  11.2 1.2 copy-done.1
  12.5 0.1 copy.26
  12.6 0.2 convert_reduce_fusion
  12.7 0.1 reduce_window_sum.11
  12.8 0.1 copy.28
  12.9 0.1 copy.27
  13.1 0.1 eq.64
  13.2 62.8 %all-reduce.3.cloned.1.call-done = f32[64,7168]{1,0:T(8,128)} async-done(((f32[64,7168]{1,0:T(8,128)}), f32[64,7168]{1,0:T(8,128)}) %all-reduce.3.cloned.1.call-update) | async-done | bytes 1835024 | tf_op jit(solution)/shard_map/psum | solution.py:37
  75.9 1.7 multiply_reduce_fusion
  77.7 4.5 %convolution_convert_fusion.1 = bf16[256,7168]{1,0:T(8,128)(2,1)} fusion(pred[256,64]{1,0:T(8,128)(4,1)S(1)} %bitcast.38, s32[256,64]{1,0:T(8,128)S(1)} %bitcast.37, s32[256]{0:T(256)S(1)} %eq.64, f32[64,7168]{1,0:T(8,128)} %all-reduce.3.cloned.1.call-done, f32[7168]{0:T(1024)S(1)} %copy-done.5, f32[64]{0:T(128)S(1)} %add_rsqrt_fusion), kind=kOutput, calls=%fused_computation.1 | convolution fusion | flops 238125056 | bytes 5616896 | tf_op jit(solution)/shard_map/dot_general | solution.py:43
  82.3 7.0 %reshape.39 = bf16[64,4,7168]{2,1,0:T(4,128)(2,1)} reshape(bf16[256,7168]{1,0:T(8,128)(2,1)} %convolution_convert_fusion.1) | data formatting | bytes 7340032 | tf_op jit(solution)/shard_map/reshape | solution.py:48
  89.3 94.8 %all_to_all.10 = bf16[64,4,7168]{2,1,0:T(4,128)(2,1)} all-to-all(bf16[64,4,7168]{2,1,0:T(4,128)(2,1)} %reshape.39), channel_id=1, replica_groups=mesh['dp'=64,'tp'=4] {'dp'}, dimensions={0} | all-to-all | bytes 7340032 | tf_op jit(solution)/shard_map/all_to_all | solution.py:47
  184.1 6.7 %reshape.40 = bf16[256,7168]{1,0:T(8,128)(2,1)} reshape(bf16[64,4,7168]{2,1,0:T(4,128)(2,1)} %all_to_all.10) | data formatting | bytes 7340032 | tf_op jit(solution)/shard_map/reshape | solution.py:54
  190.8 4.4 %fusion.3 = f32[256,256]{1,0:T(8,128)S(1)} fusion(bf16[256,7168]{1,0:T(8,128)(2,1)} %reshape.40, bf16[1,7168,256]{2,1,0:T(8,128)(2,1)} %param.13), kind=kOutput, calls=%fused_computation.5 | convolution fusion | flops 939524096 | bytes 7602176 | tf_op jit(solution)/shard_map/dot_general | solution.py:55
  195.2 0.9 copy-done.8
  196.1 1.7 abs_reduce_fusion.1
  197.9 0.3 copy-done.2
  198.2 2.9 convolution_convert_fusion
  201.1 40.8 %reduce-scatter.2.cloned.1.call-done = bf16[256,1792]{1,0:T(8,128)(2,1)} async-done(((bf16[256,7168]{1,0:T(8,128)(2,1)}), bf16[256,1792]{1,0:T(8,128)(2,1)}) %reduce-scatter.2.cloned.1.call-update) | async-done | bytes 917520 | tf_op jit(solution)/shard_map/reduce_scatter | solution.py:62
  241.9 2.5 convert_element_type.57
  244.4 10.6 %all-to-all-start.1 = ((bf16[64,4,1792]{2,1,0:T(4,128)(2,1)}), bf16[64,4,1792]{2,1,0:T(4,128)(2,1)S(1)}, u32[]{:S(2)}, u32[]{:S(2)}) async-start(bf16[64,4,1792]{2,1,0:T(4,128)(2,1)} %convert_element_type.57), calls=%async_computation.2 | async-start | bytes 1835008 | tf_op jit(solution)/shard_map/all_to_all | solution.py:65
  255.1 0.1 copy.29
  255.2 0.2 select_reduce_fusion
  255.5 0.4 abs_reduce_fusion
  255.9 0.1 multiply_reduce_fusion.1
  256.0 0.7 compare_select_fusion
  256.7 76.8 %all-reduce = (f32[64]{0:T(128)S(1)}, f32[64]{0:T(128)S(1)}) all-reduce(f32[64]{0:T(128)S(1)} %multiply_reduce_fusion.1, f32[64]{0:T(128)S(1)} %compare_select_fusion), channel_id=1, replica_groups=mesh['dp'=64,'tp'=4] {'dp','tp'}, use_global_device_ids=true, to_apply=%region_8.9 | all-reduce | flops 128 | bytes 1024 | tf_op jit(solution)/shard_map/pmax | solution.py:84
  333.5 0.6 dynamic_slice.18
  334.1 0.6 dynamic_slice.17
  334.7 1.3 fusion.6
  (28 shorter events, 0.4 us)
Async XLA Ops:
  7.2 2.9 copy-start.4
  7.2 68.7 %all-reduce.3.cloned.1.call-start = ((), (), s32[]{:S(2)}) async-start(), calls=%async_computation.3 | async-start | bytes 3670016 | tf_op jit(solution)/shard_map/psum | solution.py:37
  7.2 5.3 %copy-start.6 = (s32[64,8]{0,1:T(8,128)S(1)}, s32[64,8]{0,1:T(8,128)}, u32[]{:S(2)}) copy-start(s32[64,8]{0,1:T(8,128)} %param.11) | copy-start | bytes 6148
  10.1 67.7 %copy-start.5 = (f32[7168]{0:T(1024)S(1)}, f32[7168]{0:T(1024)}, u32[]{:S(2)}) copy-start(f32[7168]{0:T(1024)} %param.10) | copy-start | bytes 86020
  11.2 1.3 copy-start.1
  12.4 229.5 %reduce-scatter.2.cloned.1.call-start = ((), (), s32[]{:S(2)}) async-start(), calls=%async_computation.4 | async-start | bytes 4587520 | tf_op jit(solution)/shard_map/reduce_scatter | solution.py:62
  190.8 4.4 %copy-start.3 = (bf16[256,7168]{1,0:T(8,128)(2,1)S(1)}, bf16[256,7168]{1,0:T(8,128)(2,1)}, u32[]{:S(2)}) copy-start(bf16[256,7168]{1,0:T(8,128)(2,1)} %reshape.40) | copy-start | bytes 11010052
  190.8 5.3 %copy-start.8 = (bf16[1,7168,256]{2,1,0:T(8,128)(2,1)S(1)}, bf16[1,7168,256]{2,1,0:T(8,128)(2,1)}, u32[]{:S(2)}) copy-start(bf16[1,7168,256]{2,1,0:T(8,128)(2,1)} %param.14) | copy-start | bytes 11010052
  196.1 2.0 copy-start.2
  201.1 54.0 %copy-start.7 = (bf16[64,8]{0,1:T(8,128)(2,1)S(1)}, bf16[64,8]{0,1:T(8,128)(2,1)}, u32[]{:S(2)}) copy-start(bf16[64,8]{0,1:T(8,128)(2,1)} %param.12) | copy-start | bytes 3076
  201.1 54.4 %copy-start = (f32[64,7168]{1,0:T(8,128)S(1)}, f32[64,7168]{1,0:T(8,128)}, u32[]{:S(2)}) copy-start(f32[64,7168]{1,0:T(8,128)} %all-reduce.3.cloned.1.call-done) | copy-start | bytes 5505028
  244.4 90.2 %all-to-all-start.1 = ((bf16[64,4,1792]{2,1,0:T(4,128)(2,1)}), bf16[64,4,1792]{2,1,0:T(4,128)(2,1)S(1)}, u32[]{:S(2)}, u32[]{:S(2)}) async-start(bf16[64,4,1792]{2,1,0:T(4,128)(2,1)} %convert_element_type.57), calls=%async_computation.2 | async-start | bytes 1835008 | tf_op jit(solution)/shard_map/all_to_all | solution.py:65
Sparse Core Ops, SparseCore 0:
  12.6 63.3 all-reduce.2
  201.2 40.6 reduce-scatter.1
where the time goes:
time: 344 us; the launch traced here: 343 us
  blocking collectives  172 us (50%)
  waiting for transfers between devices  104 us (30%)
  local copies, waits for them, and re-layouts  20.5 us (6%)
  matrix products  14.9 us (4%)
  between operations  14.2 us (4%)
  starting transfers between devices  10.7 us (3%)
  other arithmetic  7.3 us (2%)
    all_to_all x1, blocking collectives, on_device(): lax.all_to_all(outgoing.reshape(experts, EXPERT_SLOTS, piece_width), 'dp'...  94.8 us
    pmax x1, blocking collectives, on_device(): lax.pmax((local_entry, hidden_local), ('dp', 'tp'))  76.8 us
    psum x1, waiting for transfers between devices, on_device(): residual = lax.psum(summand, 'tp')  62.8 us
    reduce_scatter x1, waiting for transfers between devices, on_device(): lax.psum_scatter(partial_out.astype(jnp.bfloat16), 'tp', scatter_dimensio...  40.8 us
    all_to_all x1, starting transfers between devices, on_device(): lax.all_to_all(expert_cols.reshape(experts, EXPERT_SLOTS, columns).astype...  10.6 us
    reshape x1, local copies, waits for them, and re-layouts, on_device(): outgoing.reshape(experts, EXPERT_SLOTS, piece_width)  7 us
  transfers between devices with their start and end apart: 3, of which 2 were waited for; matrix products, arithmetic and copies ran while one was open for 1% of the time, Pallas kernels for 0%

commit v1 on v0

v1 whole, which is shorter than its diff:
```python
import jax
import jax.numpy as jnp
from jax import lax
from jax.sharding import PartitionSpec as P

SLOTS = 4
eps = 1e-06


def on_device(attn_partial, hidden_in, norm_gain, expert_ids, route_prob, w_gate, w_up, w_down):
    experts = lax.axis_size("dp")
    tps = lax.axis_size("tp")
    tp_index = lax.axis_index("tp")
    tokens, columns = hidden_in.shape
    width = tps * columns
    pieces = jnp.swapaxes(attn_partial[0].reshape(tokens, tps, columns), 0, 1)
    pieces = lax.all_to_all(pieces, "tp", split_axis=0, concat_axis=0, tiled=True)
    residual = hidden_in.astype(jnp.float32) + jnp.sum(pieces.astype(jnp.float32), axis=0)
    square = lax.psum(jnp.sum(residual * residual, axis=1, keepdims=True), "tp")
    gain = lax.dynamic_slice_in_dim(norm_gain, tp_index * columns, columns, 0)
    normed = (residual * lax.rsqrt(square / width + eps) * gain).astype(jnp.bfloat16)

    matches = expert_ids[:, :, None] == jnp.arange(experts, dtype=jnp.int32)[None, None, :]
    named = jnp.any(matches, axis=1)
    weight = jnp.sum(jnp.where(matches, route_prob[:, :, None].astype(jnp.float32), 0.0), axis=1)
    earlier = jnp.tri(tokens, tokens, -1, dtype=jnp.bfloat16)
    before = jnp.dot(earlier, named.astype(jnp.bfloat16), preferred_element_type=jnp.float32)
    slot = jnp.arange(SLOTS, dtype=jnp.float32)[None, :, None]
    placing = named.T[:, None, :] & (before.T[:, None, :] == slot)
    selection = placing.reshape(experts * SLOTS, tokens).astype(jnp.bfloat16)
    combine = (placing.astype(jnp.float32) * weight.T[:, None, :]).reshape(experts * SLOTS, tokens)

    outgoing = jnp.dot(selection, normed, preferred_element_type=jnp.float32).astype(jnp.bfloat16)
    rows = lax.all_to_all(
        outgoing.reshape(experts, SLOTS, columns), "dp", split_axis=0, concat_axis=0, tiled=True
    ).reshape(experts * SLOTS, columns)
    rows = lax.all_gather(rows, "tp", axis=0, tiled=False)
    gate = sum(jnp.dot(rows[i], w_gate[0][i * columns:(i + 1) * columns], preferred_element_type=jnp.float32) for i in range(tps))
    up = sum(jnp.dot(rows[i], w_up[0][i * columns:(i + 1) * columns], preferred_element_type=jnp.float32) for i in range(tps))
    act = (jax.nn.silu(gate) * up).astype(jnp.bfloat16)
    partial = jnp.dot(act, w_down[0], preferred_element_type=jnp.float32).astype(jnp.bfloat16)
    amax_input = jnp.max(jnp.abs(rows)).astype(jnp.float32).reshape(1)
    amax_hidden = lax.pmax(jnp.max(jnp.abs(act)).astype(jnp.float32).reshape(1), "tp")
    out = lax.psum_scatter(partial, "tp", scatter_dimension=1, tiled=True)
    back = lax.all_to_all(
        out.reshape(experts, SLOTS, columns), "dp", split_axis=0, concat_axis=0, tiled=True
    ).reshape(experts * SLOTS, columns)
    moe = jnp.dot(combine.T, back.astype(jnp.float32), precision=lax.Precision.HIGHEST, preferred_element_type=jnp.float32)
    return (residual + moe).astype(jnp.bfloat16), amax_input, amax_hidden


def solution(mesh):
    placed = (
        P("tp", "dp", None),
        P("dp", "tp"),
        P(),
        P("dp", None),
        P("dp", None),
        P("dp", None, "tp"),
        P("dp", None, "tp"),
        P("dp", "tp", None),
    )
    return jax.shard_map(
        on_device,
        mesh=mesh,
        in_specs=placed,
        out_specs=(P("dp", "tp"), P("dp"), P("dp")),
        check_vma=False,
    )
```

time: 344 us -> 226 us (0.66)
  blocking collectives: 172 us -> 56.2 us
  local copies, waits for them, and re-layouts: 20.5 us -> 8.42 us
  waiting for transfers between devices: 104 us -> 111 us
  starting transfers between devices: 10.7 us -> 15.5 us
    pmax x1, blocking collectives: 76.8 us -> 7.8 us  [on_device(): lax.pmax(jnp.max(jnp.abs(act)).astype(jnp.float32).reshape(1), 'tp')]
    psum x1 -> x0, waiting for transfers between devices: 62.8 us -> none  [on_device(): residual = lax.psum(summand, 'tp')]
    all_to_all x1, blocking collectives: 94.8 us -> 41.6 us  [on_device(): lax.all_to_all(outgoing.reshape(experts, SLOTS, columns), 'dp', split_axi...]
    all_gather x0 -> x1, waiting for transfers between devices: none -> 41.5 us  [on_device(): rows = lax.all_gather(rows, 'tp', axis=0, tiled=False)]
    all_to_all x1 -> x2, waiting for transfers between devices: 0.01 us -> 23.6 us  [the longest x1 13.2 us: on_device(): lax.all_to_all(out.reshape(experts, SLOTS, columns), 'dp', split_axis=0,...]
    reshape x2, local copies, waits for them, and re-layouts: 13.7 us -> 2.73 us  [the longest x1 2.52 us: on_device(): out.reshape(experts, SLOTS, columns)]
    psum x0 -> x1, blocking collectives: none -> 6.88 us  [on_device(): square = lax.psum(jnp.sum(residual * residual, axis=1, keepdims=True), 'tp')]
    all_to_all x1 -> x2, starting transfers between devices: 10.6 us -> 15.5 us  [the longest x1 10.6 us: on_device(): lax.all_to_all(out.reshape(experts, SLOTS, columns), 'dp', split_axis=0,...]
  transfers between devices with their start and end apart: 3 -> 4, of which waited for: 2 -> 4; matrix products, arithmetic and copies ran while one was open for 1% -> 2% of each run, Pallas kernels for 0% -> 0%
where the time goes in v1:
time: 226 us
  waiting for transfers between devices  111 us (49%)
  blocking collectives  56.2 us (25%)
  between operations  16 us (7%)
  starting transfers between devices  15.5 us (7%)
  matrix products  15.2 us (7%)
  local copies, waits for them, and re-layouts  8.42 us (4%)
  other arithmetic  3.88 us (2%)
    reduce_scatter x1, waiting for transfers between devices, on_device(): out = lax.psum_scatter(partial, 'tp', scatter_dimension=1, tiled=True)  45.6 us
    all_to_all x1, blocking collectives, on_device(): lax.all_to_all(outgoing.reshape(experts, SLOTS, columns), 'dp', split_axi...  41.6 us
    all_gather x1, waiting for transfers between devices, on_device(): rows = lax.all_gather(rows, 'tp', axis=0, tiled=False)  41.5 us
    all_to_all x1, waiting for transfers between devices, on_device(): lax.all_to_all(out.reshape(experts, SLOTS, columns), 'dp', split_axis=0,...  13.2 us
    all_to_all x1, starting transfers between devices, on_device(): lax.all_to_all(out.reshape(experts, SLOTS, columns), 'dp', split_axis=0,...  10.6 us
    all_to_all x1, waiting for transfers between devices, on_device(): lax.all_to_all(pieces, 'tp', split_axis=0, concat_axis=0, tiled=True)  10.4 us
    dot_general x4, matrix products, on_device(): jnp.dot(rows[i], w_up[0][i * columns:(i + 1) * columns], preferred_elemen...  8.57 us
    pmax x1, blocking collectives, on_device(): lax.pmax(jnp.max(jnp.abs(act)).astype(jnp.float32).reshape(1), 'tp')  7.8 us
  transfers between devices with their start and end apart: 4, of which 4 were waited for; matrix products, arithmetic and copies ran while one was open for 2% of the time, Pallas kernels for 0%

profile of v1, /device:TPU:1, one launch (start us, length us, event | category | flops | bytes accessed | tf_op | source)
XLA Modules:
  0.0 225.9 jit_solution(15172562748056296158)
XLA Ops:
  7.2 2.2 reshape_squeeze.3
  9.4 1.0 copy.28
  10.4 4.8 %all-to-all-start = ((bf16[4,64,1792]{2,1,0:T(8,128)(2,1)}), bf16[4,64,1792]{2,1,0:T(8,128)(2,1)S(1)}, u32[]{:S(2)}, u32[]{:S(2)}) async-start(bf16[4,64,1792]{2,1,0:T(8,128)(2,1)} %copy.28), calls=%async_computation | async-start | bytes 1835008 | tf_op jit(solution)/shard_map/all_to_all | solution.py:17
  15.3 0.2 fusion.24
  15.7 0.8 dynamic_slice.3
  16.5 0.2 fusion.33
  16.7 10.4 %all-to-all-done = bf16[4,64,1792]{2,1,0:T(8,128)(2,1)S(1)} async-done(((bf16[4,64,1792]{2,1,0:T(8,128)(2,1)}), bf16[4,64,1792]{2,1,0:T(8,128)(2,1)S(1)}, u32[]{:S(2)}, u32[]{:S(2)}) %all-to-all-start) | async-done | bytes 917536 | tf_op jit(solution)/shard_map/all_to_all | solution.py:17
  27.1 0.1 convert_reduce_fusion
  27.2 0.2 multiply_reduce_fusion
  27.4 6.9 %psum.7 = f32[64,1]{0,1:T(1,128)S(1)} all-reduce(f32[64,1]{0,1:T(1,128)S(1)} %bitcast.71), channel_id=1, replica_groups=mesh['dp'=64,'tp'=4] {'tp'}, use_global_device_ids=true, to_apply=%region_4.5 | all-reduce | flops 64 | bytes 512 | tf_op jit(solution)/shard_map/psum | solution.py:19
  34.4 0.5 convolution_convert_fusion.1
  34.8 0.2 reshape.45
  35.1 41.6 %all_to_all.15 = bf16[64,4,1792]{2,1,0:T(4,128)(2,1)S(1)} all-to-all(bf16[64,4,1792]{2,1,0:T(4,128)(2,1)S(1)} %reshape.45), channel_id=1, replica_groups=mesh['dp'=64,'tp'=4] {'dp'}, dimensions={0} | all-to-all | bytes 1835008 | tf_op jit(solution)/shard_map/all_to_all | solution.py:34
  76.6 1.1 all_gather_reshape.3
  77.8 41.5 %all-gather.2.cloned.1.call-done = bf16[4,256,1792]{2,1,0:T(8,128)(2,1)} async-done(((bf16[1,256,1792]{2,1,0:T(8,128)(2,1)}), bf16[4,256,1792]{2,1,0:T(8,128)(2,1)}) %all-gather.2.cloned.1.call-update) | async-done | bytes 3670032 | tf_op jit(solution)/shard_map/all_gather | solution.py:37
  119.3 2.0 fusion.8
  121.3 2.5 %convolution_add_fusion.2 = f32[256,256]{1,0:T(8,128)S(1)} fusion(f32[256,256]{1,0:T(8,128)S(1)} %fusion.8, bf16[1,7168,256]{2,1,0:T(8,128)(2,1)} %param.14, bf16[4,256,1792]{2,1,0:T(8,128)(2,1)} %all-gather.2.cloned.1.call-done), kind=kOutput, calls=%fused_computation.10 | convolution fusion | flops 234946560 | bytes 2359296 | tf_op jit(solution)/shard_map/dot_general | solution.py:39
  123.9 1.6 convolution_add_fusion.1
  125.5 0.4 fusion.13
  125.9 0.4 convolution_add_fusion.5
  126.3 0.4 convolution_add_fusion.4
  126.8 0.4 convolution_add_fusion.3
  127.2 2.4 %abs_reduce_fusion.1 = (bf16[]{:T(256)}, bf16[256,256]{1,0:T(8,128)(2,1)S(1)}) fusion(f32[256,256]{1,0:T(8,128)S(1)} %convolution_add_fusion.1, bf16[1,7168,256]{2,1,0:T(8,128)(2,1)} %param.14, bf16[4,256,1792]{2,1,0:T(8,128)(2,1)S(1)} %copy-done.1, f32[256,256]{1,0:T(8,128)S(1)} %convolution_add_fusion.3), kind=kOutput, calls=%fused_computation.48 | convolution fusion | flops 235470848 | bytes 2490370 | tf_op jit(solution)/shard_map/dot_general | solution.py:39
  129.6 3.0 %convolution_convert_fusion = bf16[256,7168]{1,0:T(8,128)(2,1)} fusion(bf16[256,256]{1,0:T(8,128)(2,1)S(1)} %get-tuple-element.4, bf16[1,256,7168]{2,1,0:T(8,128)(2,1)S(1)} %copy-done), kind=kOutput, calls=%fused_computation | convolution fusion | flops 941359104 | bytes 7471104 | tf_op jit(solution)/shard_map/dot_general | solution.py:41
  132.6 45.6 %reduce-scatter.2.cloned.1.call-done = bf16[256,1792]{1,0:T(8,128)(2,1)} async-done(((bf16[256,7168]{1,0:T(8,128)(2,1)}), bf16[256,1792]{1,0:T(8,128)(2,1)}) %reduce-scatter.2.cloned.1.call-update) | async-done | bytes 917520 | tf_op jit(solution)/shard_map/reduce_scatter | solution.py:44
  178.2 2.5 %reshape.46 = bf16[64,4,1792]{2,1,0:T(4,128)(2,1)} reshape(bf16[256,1792]{1,0:T(8,128)(2,1)} %reduce-scatter.2.cloned.1.call-done) | data formatting | bytes 1835008 | tf_op jit(solution)/shard_map/reshape | solution.py:46
  180.7 10.6 %all-to-all-start.2 = ((bf16[64,4,1792]{2,1,0:T(4,128)(2,1)}), bf16[64,4,1792]{2,1,0:T(4,128)(2,1)S(1)}, u32[]{:S(2)}, u32[]{:S(2)}) async-start(bf16[64,4,1792]{2,1,0:T(4,128)(2,1)} %reshape.46), calls=%async_computation.3 | async-start | bytes 1835008 | tf_op jit(solution)/shard_map/all_to_all | solution.py:45
  191.4 0.2 select_reduce_fusion
  191.8 7.8 %pmax.7 = f32[1]{0:T(128)} all-reduce(bf16[1]{0:T(256)(128)(2,1)} %bitcast.24), channel_id=1, replica_groups=mesh['dp'=64,'tp'=4] {'tp'}, use_global_device_ids=true, to_apply=%region_8.9 | all-reduce | flops 1 | bytes 6 | tf_op jit(solution)/shard_map/pmax | solution.py:43
  199.6 3.1 %abs_reduce_fusion = bf16[]{:T(256)} fusion(bf16[4,256,1792]{2,1,0:T(8,128)(2,1)} %all-gather.2.cloned.1.call-done), kind=kLoop, calls=%fused_computation.2 | loop fusion | flops 3670015 | bytes 3670018 | tf_op jit(solution)/shard_map/reduce_max | solution.py:42
  203.4 13.2 %all-to-all-done.2 = bf16[64,4,1792]{2,1,0:T(4,128)(2,1)S(1)} async-done(((bf16[64,4,1792]{2,1,0:T(4,128)(2,1)}), bf16[64,4,1792]{2,1,0:T(4,128)(2,1)S(1)}, u32[]{:S(2)}, u32[]{:S(2)}) %all-to-all-start.2) | async-done | bytes 917536 | tf_op jit(solution)/shard_map/all_to_all | solution.py:45
  216.6 1.3 fusion.2
  (27 shorter events, 0.7 us)
Async XLA Ops:
  7.2 8.1 %copy-start.3 = (s32[64,8]{0,1:T(8,128)S(1)}, s32[64,8]{0,1:T(8,128)}, u32[]{:S(2)}) copy-start(s32[64,8]{0,1:T(8,128)} %param.11) | copy-start | bytes 6148
  7.2 20.1 %copy-start.2 = (bf16[64,1792]{1,0:T(8,128)(2,1)S(1)}, bf16[64,1792]{1,0:T(8,128)(2,1)}, u32[]{:S(2)}) copy-start(bf16[64,1792]{1,0:T(8,128)(2,1)} %param.9) | copy-start | bytes 688132
  10.4 16.7 %all-to-all-start = ((bf16[4,64,1792]{2,1,0:T(8,128)(2,1)}), bf16[4,64,1792]{2,1,0:T(8,128)(2,1)S(1)}, u32[]{:S(2)}, u32[]{:S(2)}) async-start(bf16[4,64,1792]{2,1,0:T(8,128)(2,1)} %copy.28), calls=%async_computation | async-start | bytes 1835008 | tf_op jit(solution)/shard_map/all_to_all | solution.py:17
  15.3 104.1 %all-gather.2.cloned.1.call-start = ((), (), s32[]{:S(2)}) async-start(), calls=%async_computation.4 | async-start | bytes 4587520 | tf_op jit(solution)/shard_map/all_gather | solution.py:37
  77.8 100.4 %reduce-scatter.2.cloned.1.call-start = ((), (), s32[]{:S(2)}) async-start(), calls=%async_computation.5 | async-start | bytes 4587520 | tf_op jit(solution)/shard_map/reduce_scatter | solution.py:44
  119.3 4.6 %copy-start.1 = (bf16[4,256,1792]{2,1,0:T(8,128)(2,1)S(1)}, bf16[4,256,1792]{2,1,0:T(8,128)(2,1)}, u32[]{:S(2)}) copy-start(bf16[4,256,1792]{2,1,0:T(8,128)(2,1)} %all-gather.2.cloned.1.call-done) | copy-start | bytes 11010052
  119.3 6.2 %copy-start.5 = (bf16[1,7168,256]{2,1,0:T(8,128)(2,1)S(1)}, bf16[1,7168,256]{2,1,0:T(8,128)(2,1)}, u32[]{:S(2)}) copy-start(bf16[1,7168,256]{2,1,0:T(8,128)(2,1)} %param.13) | copy-start | bytes 11010052
  126.8 2.9 %copy-start = (bf16[1,256,7168]{2,1,0:T(8,128)(2,1)S(1)}, bf16[1,256,7168]{2,1,0:T(8,128)(2,1)}, u32[]{:S(2)}) copy-start(bf16[1,256,7168]{2,1,0:T(8,128)(2,1)} %param.15) | copy-start | bytes 11010052
  132.6 58.8 %copy-start.4 = (bf16[64,8]{0,1:T(8,128)(2,1)S(1)}, bf16[64,8]{0,1:T(8,128)(2,1)}, u32[]{:S(2)}) copy-start(bf16[64,8]{0,1:T(8,128)(2,1)} %param.12) | copy-start | bytes 3076
  180.7 35.9 %all-to-all-start.2 = ((bf16[64,4,1792]{2,1,0:T(4,128)(2,1)}), bf16[64,4,1792]{2,1,0:T(4,128)(2,1)S(1)}, u32[]{:S(2)}, u32[]{:S(2)}) async-start(bf16[64,4,1792]{2,1,0:T(4,128)(2,1)} %reshape.46), calls=%async_computation.3 | async-start | bytes 1835008 | tf_op jit(solution)/shard_map/all_to_all | solution.py:45
Sparse Core Ops, SparseCore 0:
  77.9 41.3 all-gather.1
  132.7 45.3 reduce-scatter.1

commit v2 on v1

v2 whole, which is shorter than its diff:
```python
import jax
import jax.numpy as jnp
from jax import lax
from jax.experimental import pallas as pl
from jax.experimental.pallas import tpu as pltpu
from jax.sharding import PartitionSpec as P

MESH = pl.DeviceIdType.MESH
SLOTS = 4
EPS = 1e-06
NZ, NY, TPS = 8, 4, 4
CHIPS = NZ * NY
BLOCK = 2 * SLOTS
ROWS = CHIPS * BLOCK
CHUNKS = 4
PER = CHIPS // CHUNKS
CROWS = ROWS // CHUNKS
HALF = CROWS // 2
F32, BF16 = jnp.float32, jnp.bfloat16


def body(
    ids, prob, attn, hidden, gain, wg, wu, wd,
    out, amax_in, amax_hid,
    hid_v, gain_v, wg_v, wu_v, wd_v, local_sem,
    route, route_sem,
    ar, af, a_send, a_recv,
    res, sq, sq_send, sq_recv,
    nb, nb_sem, select, combine,
    og, rows, d_send, d_recv,
    g_send, g_recv,
    act, own, pb, rf, rs, fs, r_send, r_recv,
    oq, back, b_send, b_recv,
    mo, mr, m_sem,
    hm, h_send, h_recv, peak,
):
    me, t = lax.axis_index("dp"), lax.axis_index("tp")
    c, chip = lax.rem(me, 2), lax.div(me, 2)
    z, y = lax.div(chip, NY), lax.rem(chip, NY)
    tokens, width = attn.shape
    cols = width // TPS
    right, left, far = lax.rem(t + 1, TPS), lax.rem(t + 3, TPS), lax.rem(t + 2, TPS)
    mate = chip * 2 + 1 - c

    def step_of(d):
        m, dy = lax.div(d, NY), lax.rem(d, NY)
        odd = lax.rem(m, 2)
        dz = odd * lax.div(m + 1, 2) + (1 - odd) * lax.rem(NZ - lax.div(m, 2), NZ)
        return dz, dy

    def ahead(d):
        dz, dy = step_of(d)
        return (lax.rem(z + dz, NZ) * NY + lax.rem(y + dy, NY)) * 2 + c

    def behind(d):
        dz, dy = step_of(d)
        return (lax.rem(z + NZ - dz, NZ) * NY + lax.rem(y + NY - dy, NY)) * 2 + c

    def remote(src, dst, ssem, rsem, dp, tp):
        return pltpu.make_async_remote_copy(
            src_ref=src, dst_ref=dst, send_sem=ssem, recv_sem=rsem,
            device_id=(dp, tp), device_id_type=MESH,
        )

    def quarter(q):
        return pl.ds(pl.multiple_of(q * cols, 128), cols)

    def block(d):
        return pl.ds(pl.multiple_of(d * BLOCK, BLOCK), BLOCK)

    barrier = pltpu.get_barrier_semaphore()

    def greet(d, carry):
        pl.semaphore_signal(barrier, inc=1, device_id=(ahead(d), t), device_id_type=MESH)
        return carry

    for r in range(1, TPS):
        pl.semaphore_signal(barrier, inc=1, device_id=(me, lax.rem(t + r, TPS)), device_id_type=MESH)
    pl.semaphore_signal(barrier, inc=1, device_id=(mate, t), device_id_type=MESH)
    lax.fori_loop(1, CHIPS, greet, 0)

    loads = [
        pltpu.make_async_copy(attn.at[:, quarter(t)], ar.at[3], local_sem.at[0]),
        pltpu.make_async_copy(hidden, hid_v, local_sem.at[1]),
        pltpu.make_async_copy(gain.at[:, quarter(t)], gain_v, local_sem.at[2]),
        pltpu.make_async_copy(wg, wg_v, local_sem.at[3]),
        pltpu.make_async_copy(wu, wu_v, local_sem.at[4]),
        pltpu.make_async_copy(wd, wd_v, local_sem.at[5]),
    ]
    for load in loads:
        load.start()

    lane = lax.broadcasted_iota(jnp.int32, (8, 128), 1)
    mine = (lane >> 6) == c
    idf, prf = ids[...].astype(F32), prob[...].astype(F32)
    route[c, 0:8, :] = jnp.where(mine, jnp.concatenate([idf, idf], axis=1), 0.0)
    route[c, 8:16, :] = jnp.where(mine, jnp.concatenate([prf, prf], axis=1), 0.0)

    pl.semaphore_wait(barrier, CHIPS - 1 + 1 + TPS - 1)

    h = tokens // 2
    exchange = [
        remote(attn.at[0:h, quarter(far)], af.at[0], a_send.at[0], a_recv.at[0], me, right),
        remote(attn.at[h:tokens, quarter(far)], af.at[1], a_send.at[1], a_recv.at[1], me, left),
        remote(attn.at[:, quarter(right)], ar.at[0], a_send.at[2], a_recv.at[2], me, right),
        remote(attn.at[:, quarter(left)], ar.at[1], a_send.at[3], a_recv.at[3], me, left),
    ]
    for e in exchange:
        e.start()
    routes = remote(route.at[c], route.at[c], route_sem.at[0], route_sem.at[1], mate, t)
    routes.start()
    onward = [
        remote(af.at[0], ar.at[2, 0:h], a_send.at[4], a_recv.at[4], me, right),
        remote(af.at[1], ar.at[2, h:tokens], a_send.at[5], a_recv.at[5], me, left),
    ]
    for i in range(2):
        exchange[i].wait_recv()
        onward[i].start()

    routes.wait_recv()
    both = route[0] + route[1]
    j = lax.broadcasted_iota(jnp.int32, (ROWS, 128), 0)
    tok = lax.broadcasted_iota(jnp.int32, (ROWS, 128), 1)
    d, slot = j >> 3, j & 3
    m, dy = d >> 2, d & 3
    dz = jnp.where((m & 1) == 1, (m + 1) >> 1, (NZ - (m >> 1)) & (NZ - 1))
    expert = ((((z + dz) & (NZ - 1)) * NY + ((y + dy) & (NY - 1))) * 2 + c).astype(F32)
    weight = jnp.zeros((ROWS, 128), F32)
    match = jnp.zeros((ROWS, 128), F32)
    for k in range(8):
        hit = both[k:k + 1, :] == expert
        match = jnp.where(hit, 1.0, match)
        weight = jnp.where(hit, both[8 + k:9 + k, :], weight)
    a, b = lax.broadcasted_iota(jnp.int32, (128, 128), 0), lax.broadcasted_iota(jnp.int32, (128, 128), 1)
    earlier = jnp.where((a < b) & ((a >> 6) == (b >> 6)), 1.0, 0.0).astype(BF16)
    before = jnp.dot(match.astype(BF16), earlier, preferred_element_type=F32)
    placed = jnp.where((before == slot.astype(F32)) & (((j >> 2) & 1) == (tok >> 6)), match, 0.0)
    select[...] = placed.astype(BF16)
    combine[...] = jnp.transpose(placed * weight).astype(BF16)

    for i in range(3):
        loads[i].wait()
    exchange[2].wait_recv()
    exchange[3].wait_recv()
    onward[0].wait_recv()
    onward[1].wait_recv()
    tile = 256
    squares = jnp.zeros((tokens, tile), F32)
    for i in range(cols // tile):
        s = slice(i * tile, (i + 1) * tile)
        v = hid_v[:, s].astype(F32)
        for q in range(4):
            v = v + ar[q, :, s].astype(F32)
        res[:, s] = v
        squares = squares + v * v
    sq[0] = jnp.broadcast_to(jnp.sum(squares, axis=1, keepdims=True), (tokens, 128))
    share = [
        remote(sq.at[0], sq.at[r], sq_send.at[r - 1], sq_recv.at[r - 1], me, lax.rem(t + r, TPS))
        for r in range(1, TPS)
    ]
    for s in share:
        s.start()
    for s in share:
        s.wait_recv()
    inv = lax.rsqrt((sq[0] + sq[1] + sq[2] + sq[3]) / width + EPS)
    here = pl.ds(pl.multiple_of(c * tokens, tokens), tokens)
    there = pl.ds(pl.multiple_of((1 - c) * tokens, tokens), tokens)
    for i in range(cols // 128):
        s = slice(i * 128, (i + 1) * 128)
        nb[here, s] = (res[:, s] * inv * gain_v[:, s]).astype(BF16)
    swap = remote(nb.at[here], nb.at[here], nb_sem.at[0], nb_sem.at[1], mate, t)
    swap.start()
    swap.wait_recv()

    def outward(d):
        return remote(og.at[block(d)], rows.at[0, block(d)], d_send.at[d], d_recv.at[d], ahead(d), t)

    keep = pltpu.make_async_copy(og.at[0:BLOCK], rows.at[0, 0:BLOCK], d_recv.at[0])

    def go(d, carry):
        outward(d).start()
        return carry

    for k in range(CHUNKS):
        r = slice(k * CROWS, (k + 1) * CROWS)
        og[r, :] = jnp.dot(select[r, :], nb[...], preferred_element_type=F32).astype(BF16)
        if k == 0:
            keep.start()
        lax.fori_loop(max(1, k * PER), (k + 1) * PER, go, 0)

    def arrive(d, carry):
        outward(d).wait_recv()
        return carry

    def gather(k):
        r = slice(k * CROWS, (k + 1) * CROWS)
        lo, hi = slice(k * CROWS, k * CROWS + HALF), slice(k * CROWS + HALF, (k + 1) * CROWS)
        return [
            remote(rows.at[0, r], rows.at[1, r], g_send.at[k, 0], g_recv.at[k, 0], me, right),
            remote(rows.at[0, r], rows.at[3, r], g_send.at[k, 1], g_recv.at[k, 1], me, left),
            remote(rows.at[1, lo], rows.at[2, lo], g_send.at[k, 2], g_recv.at[k, 2], me, right),
            remote(rows.at[3, hi], rows.at[2, hi], g_send.at[k, 3], g_recv.at[k, 3], me, left),
        ]

    gathers = [gather(k) for k in range(CHUNKS)]

    def fetch(k):
        if k == 0:
            keep.wait()
        lax.fori_loop(max(1, k * PER), (k + 1) * PER, arrive, 0)
        gathers[k][0].start()
        gathers[k][1].start()

    def pass_on(k):
        gathers[k][0].wait_recv()
        gathers[k][2].start()
        gathers[k][1].wait_recv()
        gathers[k][3].start()

    def row_peak(k):
        r = slice(k * CROWS, (k + 1) * CROWS)
        top = peak[0]
        for q in range(4):
            for i in range(cols // 256):
                v = jnp.abs(rows[q, r, i * 256:(i + 1) * 256].astype(F32))
                top = jnp.maximum(top, jnp.max(v.reshape(CROWS // 8, 8, 256), axis=0))
        peak[0] = top

    def hidden_rows(k):
        r = slice(k * CROWS, (k + 1) * CROWS)
        g = jnp.zeros((CROWS, wg_v.shape[1]), F32)
        u = jnp.zeros((CROWS, wu_v.shape[1]), F32)
        for q, src in ((0, t), (1, left), (2, far), (3, right)):
            w = pl.ds(pl.multiple_of(src * cols, 256), cols)
            x = rows[q, r, :]
            g = g + jnp.dot(x, wg_v[w, :], preferred_element_type=F32)
            u = u + jnp.dot(x, wu_v[w, :], preferred_element_type=F32)
        v = (g / (1.0 + jnp.exp(-g)) * u).astype(BF16)
        act[r, :] = v
        v = jnp.abs(v.astype(F32))
        peak[1] = jnp.maximum(peak[1], jnp.max(v.reshape(CROWS // 8, 8, v.shape[1]), axis=0))

    def down(k):
        r = slice(k * CROWS, (k + 1) * CROWS)
        x = act[r, :]
        for i, dst in ((1, far), (0, right), (2, left)):
            pb[i, r, :] = jnp.dot(x, wd_v[:, quarter(dst)], preferred_element_type=F32).astype(BF16)
        own[r, :] = jnp.dot(x, wd_v[:, quarter(t)], preferred_element_type=F32)

    peak[...] = jnp.zeros(peak.shape, F32)

    def finish_gather(k):
        gathers[k][2].wait_recv()
        gathers[k][3].wait_recv()
        hidden_rows(k)
        down(k)

    def reduce(k):
        r0 = k * CROWS
        lo, hi = slice(r0, r0 + HALF), slice(r0 + HALF, r0 + CROWS)
        f = slice(k * HALF, (k + 1) * HALF)
        return [
            remote(pb.at[1, lo], rf.at[0, f], r_send.at[k, 0], r_recv.at[k, 0], me, right),
            remote(pb.at[1, hi], rf.at[1, f], r_send.at[k, 1], r_recv.at[k, 1], me, left),
            remote(pb.at[0, hi], rs.at[0, hi], r_send.at[k, 2], r_recv.at[k, 2], me, right),
            remote(pb.at[2, lo], rs.at[1, lo], r_send.at[k, 3], r_recv.at[k, 3], me, left),
            remote(fs.at[0, f], rs.at[0, lo], r_send.at[k, 4], r_recv.at[k, 4], me, right),
            remote(fs.at[1, f], rs.at[1, hi], r_send.at[k, 5], r_recv.at[k, 5], me, left),
        ]

    reduces = [reduce(k) for k in range(CHUNKS)]

    def first_hop(k):
        for i in range(4):
            reduces[k][i].start()

    def second_hop(k):
        r0 = k * CROWS
        f = slice(k * HALF, (k + 1) * HALF)
        reduces[k][0].wait_recv()
        fs[0, f] = (rf[0, f].astype(F32) + pb[0, r0:r0 + HALF].astype(F32)).astype(BF16)
        reduces[k][4].start()
        reduces[k][1].wait_recv()
        fs[1, f] = (rf[1, f].astype(F32) + pb[2, r0 + HALF:r0 + CROWS].astype(F32)).astype(BF16)
        reduces[k][5].start()

    def homeward(d):
        return remote(oq.at[block(d)], back.at[block(d)], b_send.at[d], b_recv.at[d], behind(d), t)

    stay = pltpu.make_async_copy(oq.at[0:BLOCK], back.at[0:BLOCK], b_recv.at[0])

    def go_home(d, carry):
        homeward(d).start()
        return carry

    def send_back(k):
        r = slice(k * CROWS, (k + 1) * CROWS)
        for i in range(2, 6):
            reduces[k][i].wait_recv()
        oq[r, :] = (own[r, :] + rs[0, r].astype(F32) + rs[1, r].astype(F32)).astype(BF16)
        if k == 0:
            stay.start()
        lax.fori_loop(max(1, k * PER), (k + 1) * PER, go_home, 0)

    for k in range(CHUNKS + 2):
        if k < CHUNKS:
            fetch(k)
        if 1 <= k <= CHUNKS:
            pass_on(k - 1)
        if k == 2:
            for load in loads[3:]:
                load.wait()
        if k >= 2:
            finish_gather(k - 2)

    order = (2, 3, 1, 0)
    for i in range(CHUNKS + 2):
        if i < CHUNKS:
            first_hop(order[i])
        if 1 <= i <= CHUNKS:
            second_hop(order[i - 1])
        if i >= 2:
            send_back(order[i - 2])
        if i == 0:
            for k in range(CHUNKS):
                row_peak(k)
            hm[0] = jnp.broadcast_to(jnp.max(peak[1]), (8, 128))
            tops = [
                remote(hm.at[0], hm.at[r], h_send.at[r - 1], h_recv.at[r - 1], me, lax.rem(t + r, TPS))
                for r in range(1, TPS)
            ]
            for s in tops:
                s.start()
            amax_in[0] = jnp.max(peak[0])

    def returned(d, carry):
        homeward(d).wait_recv()
        return carry

    for s in tops:
        s.wait_recv()
    amax_hid[0] = jnp.max(jnp.maximum(jnp.maximum(hm[0], hm[1]), jnp.maximum(hm[2], hm[3])))
    stay.wait()
    lax.fori_loop(1, CHIPS, returned, 0)
    mo[...] = jnp.dot(combine[there, :], back[...], preferred_element_type=F32)
    give = remote(mo, mr, m_sem.at[0], m_sem.at[1], mate, t)
    give.start()
    res[...] = res[...] + jnp.dot(combine[here, :], back[...], preferred_element_type=F32)
    give.wait_recv()
    out[...] = (res[...] + mr[...]).astype(BF16)

    for s in (*exchange, *onward, routes, *share, swap, *tops, give):
        s.wait_send()
    for k in range(CHUNKS):
        for s in (*gathers[k], *reduces[k]):
            s.wait_send()

    def drained(d, carry):
        outward(d).wait_send()
        homeward(d).wait_send()
        return carry

    lax.fori_loop(1, CHIPS, drained, 0)


def on_device(attn_partial, hidden_in, norm_gain, expert_ids, route_prob, w_gate, w_up, w_down):
    tokens, cols = hidden_in.shape
    width, ff = w_gate.shape[1:]
    vmem, anywhere = pl.BlockSpec(memory_space=pltpu.VMEM), pl.BlockSpec(memory_space=pl.ANY)
    smem = pl.BlockSpec(memory_space=pltpu.SMEM)
    dma = pltpu.SemaphoreType.DMA
    V = pltpu.VMEM
    scratch = [
        V((tokens, cols), BF16), V((1, cols), F32), V((width, ff), BF16), V((width, ff), BF16), V((ff, width), BF16), dma((6,)),
        V((2, 16, 128), F32), dma((2,)),
        V((4, tokens, cols), BF16), V((2, tokens // 2, cols), BF16), dma((6,)), dma((6,)),
        V((tokens, cols), F32), V((4, tokens, 128), F32), dma((3,)), dma((3,)),
        V((2 * tokens, cols), BF16), dma((2,)), V((ROWS, 128), BF16), V((128, ROWS), BF16),
        V((ROWS, cols), BF16), V((4, ROWS, cols), BF16), dma((CHIPS,)), dma((CHIPS,)),
        dma((CHUNKS, 4)), dma((CHUNKS, 4)),
        V((ROWS, ff), BF16), V((ROWS, cols), F32), V((3, ROWS, cols), BF16), V((2, ROWS // 2, cols), BF16),
        V((2, ROWS, cols), BF16), V((2, ROWS // 2, cols), BF16), dma((CHUNKS, 6)), dma((CHUNKS, 6)),
        V((ROWS, cols), BF16), V((ROWS, cols), BF16), dma((CHIPS,)), dma((CHIPS,)),
        V((tokens, cols), F32), V((tokens, cols), F32), dma((2,)),
        V((4, 8, 128), F32), dma((3,)), dma((3,)), V((2, 8, 256), F32),
    ]
    return pl.pallas_call(
        body,
        out_shape=(
            jax.ShapeDtypeStruct((tokens, cols), BF16),
            jax.ShapeDtypeStruct((1,), F32),
            jax.ShapeDtypeStruct((1,), F32),
        ),
        in_specs=[vmem, vmem] + [anywhere] * 6,
        out_specs=(vmem, smem, smem),
        scratch_shapes=scratch,
        compiler_params=pltpu.CompilerParams(
            collective_id=0, has_side_effects=True, vmem_limit_bytes=56 << 20
        ),
    )(
        expert_ids.T, route_prob.T, attn_partial[0], hidden_in, norm_gain[None],
        w_gate[0], w_up[0], w_down[0],
    )


def solution(mesh):
    placed = (
        P("tp", "dp", None),
        P("dp", "tp"),
        P(),
        P("dp", None),
        P("dp", None),
        P("dp", None, "tp"),
        P("dp", None, "tp"),
        P("dp", "tp", None),
    )
    return jax.shard_map(
        on_device,
        mesh=mesh,
        in_specs=placed,
        out_specs=(P("dp", "tp"), P("dp"), P("dp")),
        check_vma=False,
    )
```

time: 226 us -> 122 us (0.54)
  Pallas kernels: 0 us -> 116 us
  waiting for transfers between devices: 111 us -> 0 us
  blocking collectives: 56.2 us -> 0 us
  starting transfers between devices: 15.5 us -> 0 us
  matrix products: 15.2 us -> 0 us
  between operations: 16 us -> 4.15 us
  local copies, waits for them, and re-layouts: 8.42 us -> 1.64 us
  other arithmetic: 3.88 us -> 0 us
    pallas_call x0 -> x1, Pallas kernels: none -> 116 us  [on_device(): pl.pallas_call(body, out_shape=(jax.ShapeDtypeStruct((tokens, cols), BF16...]
    reduce_scatter x1 -> x0, waiting for transfers between devices: 45.6 us -> none  [on_device(): out = lax.psum_scatter(partial, 'tp', scatter_dimension=1, tiled=True)]
    all_to_all x1 -> x0, blocking collectives: 41.6 us -> none  [on_device(): lax.all_to_all(outgoing.reshape(experts, SLOTS, columns), 'dp', split_axi...]
    all_gather x1 -> x0, waiting for transfers between devices: 41.5 us -> none  [on_device(): rows = lax.all_gather(rows, 'tp', axis=0, tiled=False)]
    all_to_all x2 -> x0, waiting for transfers between devices: 23.6 us -> none  [the longest x1 13.2 us: on_device(): lax.all_to_all(out.reshape(experts, SLOTS, columns), 'dp', split_axis=0,...]
    all_to_all x2 -> x0, starting transfers between devices: 15.5 us -> none  [the longest x1 10.6 us: on_device(): lax.all_to_all(out.reshape(experts, SLOTS, columns), 'dp', split_axis=0,...]
    dot_general x12 -> x0, matrix products: 15.2 us -> none  [the longest x4 8.57 us: on_device(): jnp.dot(rows[i], w_up[0][i * columns:(i + 1) * columns], preferred_elemen...]
    pmax x1 -> x0, blocking collectives: 7.8 us -> none  [on_device(): lax.pmax(jnp.max(jnp.abs(act)).astype(jnp.float32).reshape(1), 'tp')]
  transfers between devices with their start and end apart: 4 -> 0, of which waited for: 4 -> 0; matrix products, arithmetic and copies ran while one was open for 2% -> 0% of each run, Pallas kernels for 0% -> 0%
where the time goes in v2:
time: 122 us
  Pallas kernels  116 us (95%)
  between operations  4.15 us (3%)
  local copies, waits for them, and re-layouts  1.64 us (1%)
    pallas_call x1, Pallas kernels, on_device(): pl.pallas_call(body, out_shape=(jax.ShapeDtypeStruct((tokens, cols), BF16...  116 us

profile of v2, /device:TPU:1, one launch (start us, length us, event | category | flops | bytes accessed | tf_op | source)
XLA Modules:
  0.0 121.7 jit_solution(17734939873139010415)
XLA Ops:
  0.6 115.9 %shard_map.103 = (bf16[64,1792]{1,0:T(8,128)(2,1)}, f32[1]{0:T(128)}, f32[1]{0:T(128)}) custom-call(s32[8,64]{1,0:T(8,128)} %bitcast.12, bf16[8,64]{1,0:T(8,128)(2,1)} %bitcast.13, bf16[64,7168]{1,0:T(8,128)(2,1)} %bitcast.10, bf16[64,1792]{1,0:T(8,128)(2,1)} %hidden.1, f32[1,7168]{1,0:T(1,128)} %bitcast.11, bf16[7168,256]{1,0:T(8,128)(2,1)} %bitcast.7, ...), custom_call_target="tpu_custom_call" | custom-call | tf_op jit(solution)/shard_map/pallas_call | solution.py:387
  116.6 1.6 %copy.14 = bf16[64,1792]{1,0:T(8,128)(2,1)} copy(bf16[64,1792]{1,0:T(8,128)(2,1)} %get-tuple-element.6) | data formatting | bytes 458752

commit v3 on v2

v3 whole, which is shorter than its diff:
```python
import jax
import jax.numpy as jnp
from jax import lax
from jax.experimental import pallas as pl
from jax.experimental.pallas import tpu as pltpu
from jax.sharding import PartitionSpec as P

MESH = pl.DeviceIdType.MESH
SLOTS = 4
EPS = 1e-06
NZ, NY, TPS = 8, 4, 4
CHIPS = NZ * NY
BLOCK = 2 * SLOTS
ROWS = CHIPS * BLOCK
CHUNKS = 4
PER = CHIPS // CHUNKS
CROWS = ROWS // CHUNKS
HALF = CROWS // 2
F32, BF16 = jnp.float32, jnp.bfloat16
PARTS = ((0, 768), (768, 1024))
EXTRA = 128
FIRST, LAST = (0, 1, 2, 3), (2, 3, 1, 0)


def body(
    ids, prob, attn, hidden, gain, wg, wu, wd,
    out, amax_in, amax_hid,
    hid_v, gain_v, wg_v, wu_v, wd_v, local_sem, known,
    route, route_sem,
    ar, af, a_send, a_recv,
    res, sq, sq_send, sq_recv,
    nb, nb_sem, select, combine,
    og, rows, d_send, d_recv, keep_sem,
    g_send, g_recv,
    g_acc, u_acc, act, own, pb, rf, rs, fs, r_send, r_recv,
    oq, back, b_send, b_recv,
    mo, mr, m_sem,
    hm, h_send, h_recv, peak,
):
    me, t = lax.axis_index("dp"), lax.axis_index("tp")
    c, chip = lax.rem(me, 2), lax.div(me, 2)
    z, y = lax.div(chip, NY), lax.rem(chip, NY)
    tokens, width = attn.shape
    cols = width // TPS
    right, left, far = lax.rem(t + 1, TPS), lax.rem(t + 3, TPS), lax.rem(t + 2, TPS)
    mate = chip * 2 + 1 - c

    def along_z(k):
        return (lax.rem(z + k, NZ) * NY + y) * 2 + c

    def along_y(k):
        return (z * NY + lax.rem(y + k, NY)) * 2 + c

    def remote(src, dst, ssem, rsem, dp, tp):
        return pltpu.make_async_remote_copy(
            src_ref=src, dst_ref=dst, send_sem=ssem, recv_sem=rsem,
            device_id=(dp, tp), device_id_type=MESH,
        )

    def tell(sem, dp, tp):
        pl.semaphore_signal(sem, inc=1, device_id=(dp, tp), device_id_type=MESH)

    def quarter(q, start=0, size=None):
        return pl.ds(pl.multiple_of(q * cols + start, 128), cols if size is None else size)

    def block(d):
        return pl.ds(pl.multiple_of(d * BLOCK, BLOCK), BLOCK)

    barrier = pltpu.get_barrier_semaphore()
    for r in range(1, TPS):
        tell(barrier, me, lax.rem(t + r, TPS))
    tell(barrier, mate, t)
    for k in (1, NZ - 1):
        tell(barrier, along_z(k), t)
    for k in (1, NY - 1):
        tell(barrier, along_y(k), t)

    loads = [
        pltpu.make_async_copy(attn.at[:, quarter(t)], ar.at[3], local_sem.at[0]),
        pltpu.make_async_copy(hidden, hid_v, local_sem.at[1]),
        pltpu.make_async_copy(gain.at[:, quarter(t)], gain_v, local_sem.at[2]),
        pltpu.make_async_copy(wg, wg_v, local_sem.at[3]),
        pltpu.make_async_copy(wu, wu_v, local_sem.at[4]),
        pltpu.make_async_copy(wd, wd_v, local_sem.at[5]),
    ]
    for load in loads:
        load.start()

    lane = lax.broadcasted_iota(jnp.int32, (8, 128), 1)
    mine = (lane >> 6) == c
    idf, prf = ids[...].astype(F32), prob[...].astype(F32)
    route[c, 0:8, :] = jnp.where(mine, jnp.concatenate([idf, idf], axis=1), 0.0)
    route[c, 8:16, :] = jnp.where(mine, jnp.concatenate([prf, prf], axis=1), 0.0)

    pl.semaphore_wait(barrier, TPS - 1 + 1 + 4)

    h = tokens // 2

    def exchange_of(p):
        start, size = PARTS[p]
        at = pl.ds(start, size)
        return [
            remote(attn.at[0:h, quarter(far, start, size)], af.at[0, :, at], a_send.at[p, 0], a_recv.at[p, 0], me, right),
            remote(attn.at[h:tokens, quarter(far, start, size)], af.at[1, :, at], a_send.at[p, 1], a_recv.at[p, 1], me, left),
            remote(attn.at[:, quarter(right, start, size)], ar.at[0, :, at], a_send.at[p, 2], a_recv.at[p, 2], me, right),
            remote(attn.at[:, quarter(left, start, size)], ar.at[1, :, at], a_send.at[p, 3], a_recv.at[p, 3], me, left),
            remote(af.at[0, :, at], ar.at[2, 0:h, at], a_send.at[p, 4], a_recv.at[p, 4], me, right),
            remote(af.at[1, :, at], ar.at[2, h:tokens, at], a_send.at[p, 5], a_recv.at[p, 5], me, left),
        ]

    exchange = [exchange_of(p) for p in range(2)]

    def onward(p):
        for i in range(2):
            exchange[p][i].wait_recv()
            exchange[p][4 + i].start()

    for e in exchange[0][:4]:
        e.start()
    routes = remote(route.at[c], route.at[c], route_sem.at[0], route_sem.at[1], mate, t)
    routes.start()
    for k in (1, NZ - 1):
        tell(known.at[0], along_z(k), t)
    for k in (1, NY - 1):
        tell(known.at[0], along_y(k), t)
    onward(0)
    for e in exchange[1][:4]:
        e.start()
    pl.semaphore_wait(known.at[0], 4)
    for k in (2, NZ - 2):
        tell(known.at[1], along_z(k), t)

    routes.wait_recv()
    both = route[0] + route[1]
    j = lax.broadcasted_iota(jnp.int32, (ROWS, 128), 0)
    tok = lax.broadcasted_iota(jnp.int32, (ROWS, 128), 1)
    d, slot = j >> 3, j & 3
    m, dy = d >> 2, d & 3
    dz = jnp.where((m & 1) == 1, (m + 1) >> 1, (NZ - (m >> 1)) & (NZ - 1))
    expert = ((((z + dz) & (NZ - 1)) * NY + ((y + dy) & (NY - 1))) * 2 + c).astype(F32)
    weight = jnp.zeros((ROWS, 128), F32)
    match = jnp.zeros((ROWS, 128), F32)
    for k in range(8):
        hit = both[k:k + 1, :] == expert
        match = jnp.where(hit, 1.0, match)
        weight = jnp.where(hit, both[8 + k:9 + k, :], weight)
    a, b = lax.broadcasted_iota(jnp.int32, (128, 128), 0), lax.broadcasted_iota(jnp.int32, (128, 128), 1)
    earlier = jnp.where((a < b) & ((a >> 6) == (b >> 6)), 1.0, 0.0).astype(BF16)
    before = jnp.dot(match.astype(BF16), earlier, preferred_element_type=F32)
    placed = jnp.where((before == slot.astype(F32)) & (((j >> 2) & 1) == (tok >> 6)), match, 0.0)
    select[...] = placed.astype(BF16)
    weighted = placed * weight
    for k in range(CHUNKS):
        combine[k] = jnp.transpose(weighted[k * CROWS:(k + 1) * CROWS, :]).astype(BF16)

    pl.semaphore_wait(known.at[1], 2)
    for k in range(1, NY):
        tell(known.at[2], along_y(k), t)

    here = pl.ds(pl.multiple_of(c * tokens, tokens), tokens)
    there = pl.ds(pl.multiple_of((1 - c) * tokens, tokens), tokens)
    tile = 256

    def attend(p, squares):
        start, size = PARTS[p]
        for i in range(2, 6):
            exchange[p][i].wait_recv()
        for i in range(start // tile, (start + size) // tile):
            s = slice(i * tile, (i + 1) * tile)
            v = hid_v[:, s].astype(F32)
            for q in range(4):
                v = v + ar[q, :, s].astype(F32)
            res[:, s] = v
            nb[here, s] = (v * gain_v[:, s]).astype(BF16)
            squares = squares + v * v
        return squares

    def swap_of(p):
        start, size = PARTS[p]
        at = pl.ds(start, size + p * EXTRA)
        return remote(nb.at[here, at], nb.at[here, at], nb_sem.at[p, 0], nb_sem.at[p, 1], mate, t)

    def place(m):
        return (m + 1) // 2 if m % 2 else (NZ - m // 2) % NZ

    def hops(k, act_on):
        for m in (2 * k, 2 * k + 1):
            def one(dy, carry, m=m):
                act_on(m, dy)
                return carry

            lax.fori_loop(1 if m == 0 else 0, NY, one, 0)

    def outward(p, m, dy):
        start, size = PARTS[p]
        d = m * NY + dy
        at = pl.ds(start, size + p * EXTRA)
        dp = (lax.rem(z + place(m), NZ) * NY + lax.rem(y + dy, NY)) * 2 + c
        return remote(og.at[block(d), at], rows.at[0, block(d), at], d_send.at[p, d], d_recv.at[p, d], dp, t)

    def keep_of(p):
        start, size = PARTS[p]
        at = pl.ds(start, size + p * EXTRA)
        return pltpu.make_async_copy(og.at[0:BLOCK, at], rows.at[0, 0:BLOCK, at], keep_sem.at[p])

    def dispatch(p, order):
        start, size = PARTS[p]
        at = slice(start, start + size + p * EXTRA)
        for k in order:
            r = slice(k * CROWS, (k + 1) * CROWS)
            og[r, at] = jnp.dot(select[r, :], nb[:, at], preferred_element_type=F32).astype(BF16)
            if k == 0:
                keep_of(p).start()
            hops(k, lambda m, dy: outward(p, m, dy).start())

    def gather_of(p, k):
        start, size = PARTS[p]
        at = pl.ds(start, size)
        r = pl.ds(k * CROWS, CROWS)
        lo, hi = pl.ds(k * CROWS, HALF), pl.ds(k * CROWS + HALF, HALF)
        snd, rcv = [g_send.at[p, k, i] for i in range(4)], [g_recv.at[p, k, i] for i in range(4)]
        return [
            remote(rows.at[0, r, at], rows.at[1, r, at], snd[0], rcv[0], me, right),
            remote(rows.at[0, r, at], rows.at[3, r, at], snd[1], rcv[1], me, left),
            remote(rows.at[1, lo, at], rows.at[2, lo, at], snd[2], rcv[2], me, right),
            remote(rows.at[3, hi, at], rows.at[2, hi, at], snd[3], rcv[3], me, left),
        ]

    gathers = [[gather_of(p, k) for k in range(CHUNKS)] for p in range(2)]

    def fetch(p, k):
        if k == 0:
            keep_of(p).wait()
        hops(k, lambda m, dy: outward(p, m, dy).wait_recv())
        gathers[p][k][0].start()
        gathers[p][k][1].start()

    def pass_on(p, k):
        gathers[p][k][0].wait_recv()
        gathers[p][k][2].start()
        gathers[p][k][1].wait_recv()
        gathers[p][k][3].start()

    def factor(r):
        return jnp.sum(rows[0, r, cols:cols + EXTRA].astype(F32), axis=1, keepdims=True)

    def hidden_rows(p, k):
        start, size = PARTS[p]
        r = slice(k * CROWS, (k + 1) * CROWS)
        if p == 0:
            g = jnp.zeros((CROWS, wg_v.shape[1]), F32)
            u = jnp.zeros((CROWS, wu_v.shape[1]), F32)
        else:
            g, u = g_acc[r, :], u_acc[r, :]
        for q, src in ((0, t), (1, left), (2, far), (3, right)):
            w = pl.ds(pl.multiple_of(src * cols + start, 256), size)
            x = rows[q, r, start:start + size]
            g = g + jnp.dot(x, wg_v[w, :], preferred_element_type=F32)
            u = u + jnp.dot(x, wu_v[w, :], preferred_element_type=F32)
        if p == 0:
            g_acc[r, :] = g
            u_acc[r, :] = u
        else:
            f = factor(r)
            g, u = g * f, u * f
            v = (g / (1.0 + jnp.exp(-g)) * u).astype(BF16)
            act[r, :] = v
            v = jnp.abs(v.astype(F32))
            peak[...] = jnp.maximum(peak[...], jnp.max(v.reshape(CROWS // 8, 8, v.shape[1]), axis=0))

    def down(k):
        r = slice(k * CROWS, (k + 1) * CROWS)
        x = act[r, :]
        for i, dst in ((1, far), (0, right), (2, left)):
            pb[i, r, :] = jnp.dot(x, wd_v[:, quarter(dst)], preferred_element_type=F32).astype(BF16)
        own[r, :] = jnp.dot(x, wd_v[:, quarter(t)], preferred_element_type=F32)

    def reduce_of(k):
        r0 = k * CROWS
        lo, hi = pl.ds(r0, HALF), pl.ds(r0 + HALF, HALF)
        f = pl.ds(k * HALF, HALF)
        snd, rcv = [r_send.at[k, i] for i in range(6)], [r_recv.at[k, i] for i in range(6)]
        return [
            remote(pb.at[1, lo], rf.at[0, f], snd[0], rcv[0], me, right),
            remote(pb.at[1, hi], rf.at[1, f], snd[1], rcv[1], me, left),
            remote(pb.at[0, hi], rs.at[0, hi], snd[2], rcv[2], me, right),
            remote(pb.at[2, lo], rs.at[1, lo], snd[3], rcv[3], me, left),
            remote(fs.at[0, f], rs.at[0, lo], snd[4], rcv[4], me, right),
            remote(fs.at[1, f], rs.at[1, hi], snd[5], rcv[5], me, left),
        ]

    reduces = [reduce_of(k) for k in range(CHUNKS)]

    def finish(p, k):
        gathers[p][k][2].wait_recv()
        gathers[p][k][3].wait_recv()
        hidden_rows(p, k)
        if p == 1:
            down(k)
            for i in range(4):
                reduces[k][i].start()

    def second_hop(k):
        r0 = k * CROWS
        f = slice(k * HALF, (k + 1) * HALF)
        reduces[k][0].wait_recv()
        fs[0, f] = (rf[0, f].astype(F32) + pb[0, r0:r0 + HALF].astype(F32)).astype(BF16)
        reduces[k][4].start()
        reduces[k][1].wait_recv()
        fs[1, f] = (rf[1, f].astype(F32) + pb[2, r0 + HALF:r0 + CROWS].astype(F32)).astype(BF16)
        reduces[k][5].start()

    def homeward(m, dy):
        d = m * NY + dy
        dp = (lax.rem(z + NZ - place(m), NZ) * NY + lax.rem(y + NY - dy, NY)) * 2 + c
        return remote(oq.at[block(d)], back.at[block(d)], b_send.at[d], b_recv.at[d], dp, t)

    stay = pltpu.make_async_copy(oq.at[0:BLOCK], back.at[0:BLOCK], keep_sem.at[2])

    def send_back(k):
        r = slice(k * CROWS, (k + 1) * CROWS)
        for i in range(2, 6):
            reduces[k][i].wait_recv()
        oq[r, :] = (own[r, :] + rs[0, r].astype(F32) + rs[1, r].astype(F32)).astype(BF16)
        if k == 0:
            stay.start()
        hops(k, lambda m, dy: homeward(m, dy).start())

    def collect(k):
        r = slice(k * CROWS, (k + 1) * CROWS)
        if k == 0:
            stay.wait()
        hops(k, lambda m, dy: homeward(m, dy).wait_recv())
        got = jnp.dot(combine[k, there, :], back[r, :], preferred_element_type=F32)
        mo[...] = got if k == LAST[0] else mo[...] + got
        if k == LAST[-1]:
            give.start()
        res[...] = res[...] + jnp.dot(combine[k, here, :], back[r, :], preferred_element_type=F32)

    give = remote(mo, mr, m_sem.at[0], m_sem.at[1], mate, t)

    for i in range(3):
        loads[i].wait()
    squares = attend(0, jnp.zeros((tokens, tile), F32))
    swaps = [swap_of(p) for p in range(2)]
    swaps[0].start()
    onward(1)
    pl.semaphore_wait(known.at[2], NY - 1)
    swaps[0].wait_recv()
    dispatch(0, FIRST)
    squares = attend(1, squares)
    sq[0] = jnp.broadcast_to(jnp.sum(squares, axis=1, keepdims=True), (tokens, 128))
    share = [
        remote(sq.at[0], sq.at[r], sq_send.at[r - 1], sq_recv.at[r - 1], me, lax.rem(t + r, TPS))
        for r in range(1, TPS)
    ]
    for s in share:
        s.start()
    fetch(0, FIRST[0])
    for s in share:
        s.wait_recv()
    inv = lax.rsqrt((sq[0] + sq[1] + sq[2] + sq[3]) / width + EPS)
    high = inv.astype(BF16).astype(F32)
    middle = (inv - high).astype(BF16).astype(F32)
    at = lax.broadcasted_iota(jnp.int32, (tokens, EXTRA), 1)
    terms = jnp.where(at == 0, high, jnp.where(at == 1, middle, jnp.where(at == 2, inv - high - middle, 0.0)))
    nb[here, cols:cols + EXTRA] = terms.astype(BF16)
    swaps[1].start()
    fetch(0, FIRST[1])
    pass_on(0, FIRST[0])
    swaps[1].wait_recv()
    dispatch(1, LAST)
    peak[...] = jnp.zeros(peak.shape, F32)

    units = [(0, k) for k in FIRST] + [(1, k) for k in LAST]
    n = len(units)
    for i in range(2, n + 4):
        if i < n:
            fetch(*units[i])
        if i - 1 < n:
            pass_on(*units[i - 1])
        if i == 2:
            for load in loads[3:]:
                load.wait()
        if i - 3 >= CHUNKS and i - 3 < n:
            second_hop(units[i - 3][1])
        if i - 2 < n:
            finish(*units[i - 2])
        if i == n + 1:
            hm[0] = jnp.broadcast_to(jnp.max(peak[...]), (8, 128))
            tops = [
                remote(hm.at[0], hm.at[r], h_send.at[r - 1], h_recv.at[r - 1], me, lax.rem(t + r, TPS))
                for r in range(1, TPS)
            ]
            for s in tops:
                s.start()
        if i == n + 1:
            largest = jnp.zeros((CROWS, 1), F32)
            for k in range(CHUNKS):
                r = slice(k * CROWS, (k + 1) * CROWS)
                top = jnp.zeros((CROWS, 128), F32)
                for q in range(4):
                    for l in range(cols // 128):
                        top = jnp.maximum(top, jnp.abs(rows[q, r, l * 128:(l + 1) * 128].astype(F32)))
                largest = jnp.maximum(largest, jnp.max(top, axis=1, keepdims=True) * factor(r))
            amax_in[0] = jnp.max(largest)
        if i - 4 >= CHUNKS:
            send_back(units[i - 4][1])
        if i == n + 2:
            for s in tops:
                s.wait_recv()
            amax_hid[0] = jnp.max(jnp.maximum(jnp.maximum(hm[0], hm[1]), jnp.maximum(hm[2], hm[3])))
            collect(LAST[0])
    for k in LAST[1:]:
        collect(k)
    give.wait_recv()
    out[...] = (res[...] + mr[...]).astype(BF16)

    for s in (*exchange[0], *exchange[1], routes, *share, *swaps, *tops, give):
        s.wait_send()
    for k in range(CHUNKS):
        for s in (*gathers[0][k], *gathers[1][k], *reduces[k]):
            s.wait_send()

        def drain(m, dy):
            outward(0, m, dy).wait_send()
            outward(1, m, dy).wait_send()
            homeward(m, dy).wait_send()

        hops(k, drain)


def on_device(attn_partial, hidden_in, norm_gain, expert_ids, route_prob, w_gate, w_up, w_down):
    tokens, cols = hidden_in.shape
    width, ff = w_gate.shape[1:]
    vmem, anywhere = pl.BlockSpec(memory_space=pltpu.VMEM), pl.BlockSpec(memory_space=pl.ANY)
    smem = pl.BlockSpec(memory_space=pltpu.SMEM)
    dma = pltpu.SemaphoreType.DMA
    V = pltpu.VMEM
    scratch = [
        V((tokens, cols), BF16), V((1, cols), F32), V((width, ff), BF16), V((width, ff), BF16), V((ff, width), BF16), dma((6,)),
        pltpu.SemaphoreType.REGULAR((3,)),
        V((2, 16, 128), F32), dma((2,)),
        V((4, tokens, cols), BF16), V((2, tokens // 2, cols), BF16), dma((2, 6)), dma((2, 6)),
        V((tokens, cols), F32), V((4, tokens, 128), F32), dma((3,)), dma((3,)),
        V((2 * tokens, cols + EXTRA), BF16), dma((2, 2)), V((ROWS, 128), BF16), V((CHUNKS, 128, CROWS), BF16),
        V((ROWS, cols + EXTRA), BF16), V((4, ROWS, cols + EXTRA), BF16), dma((2, CHIPS)), dma((2, CHIPS)), dma((3,)),
        dma((2, CHUNKS, 4)), dma((2, CHUNKS, 4)),
        V((ROWS, ff), F32), V((ROWS, ff), F32),
        V((ROWS, ff), BF16), V((ROWS, cols), F32), V((3, ROWS, cols), BF16), V((2, ROWS // 2, cols), BF16),
        V((2, ROWS, cols), BF16), V((2, ROWS // 2, cols), BF16), dma((CHUNKS, 6)), dma((CHUNKS, 6)),
        V((ROWS, cols), BF16), V((ROWS, cols), BF16), dma((CHIPS,)), dma((CHIPS,)),
        V((tokens, cols), F32), V((tokens, cols), F32), dma((2,)),
        V((4, 8, 128), F32), dma((3,)), dma((3,)), V((8, 256), F32),
    ]
    return pl.pallas_call(
        body,
        out_shape=(
            jax.ShapeDtypeStruct((tokens, cols), BF16),
            jax.ShapeDtypeStruct((1,), F32),
            jax.ShapeDtypeStruct((1,), F32),
        ),
        in_specs=[vmem, vmem] + [anywhere] * 6,
        out_specs=(vmem, smem, smem),
        scratch_shapes=scratch,
        compiler_params=pltpu.CompilerParams(
            collective_id=0, has_side_effects=True, vmem_limit_bytes=56 << 20
        ),
    )(
        expert_ids.T, route_prob.T, attn_partial[0], hidden_in, norm_gain[None],
        w_gate[0], w_up[0], w_down[0],
    )


def solution(mesh):
    placed = (
        P("tp", "dp", None),
        P("dp", "tp"),
        P(),
        P("dp", None),
        P("dp", None),
        P("dp", None, "tp"),
        P("dp", None, "tp"),
        P("dp", "tp", None),
    )
    return jax.shard_map(
        on_device,
        mesh=mesh,
        in_specs=placed,
        out_specs=(P("dp", "tp"), P("dp"), P("dp")),
        check_vma=False,
    )
```

time: 122 us -> 110 us (0.902)
  Pallas kernels: 116 us -> 104 us
    pallas_call x1, Pallas kernels: 116 us -> 104 us  [on_device(): pl.pallas_call(body, out_shape=(jax.ShapeDtypeStruct((tokens, cols), BF16...]
where the time goes in v3:
time: 110 us
  Pallas kernels  104 us (95%)
  between operations  4.15 us (4%)
  local copies, waits for them, and re-layouts  1.64 us (1%)
    pallas_call x1, Pallas kernels, on_device(): pl.pallas_call(body, out_shape=(jax.ShapeDtypeStruct((tokens, cols), BF16...  104 us

profile of v3, /device:TPU:1, one launch (start us, length us, event | category | flops | bytes accessed | tf_op | source)
XLA Modules:
  0.0 109.9 jit_solution(7024520598674468084)
XLA Ops:
  0.6 104.1 %shard_map.103 = (bf16[64,1792]{1,0:T(8,128)(2,1)}, f32[1]{0:T(128)}, f32[1]{0:T(128)}) custom-call(s32[8,64]{1,0:T(8,128)} %bitcast.12, bf16[8,64]{1,0:T(8,128)(2,1)} %bitcast.13, bf16[64,7168]{1,0:T(8,128)(2,1)} %bitcast.10, bf16[64,1792]{1,0:T(8,128)(2,1)} %hidden.1, f32[1,7168]{1,0:T(1,128)} %bitcast.11, bf16[7168,256]{1,0:T(8,128)(2,1)} %bitcast.7, ...), custom_call_target="tpu_custom_call" | custom-call | tf_op jit(solution)/shard_map/pallas_call | solution.py:456
  104.8 1.6 %copy.14 = bf16[64,1792]{1,0:T(8,128)(2,1)} copy(bf16[64,1792]{1,0:T(8,128)(2,1)} %get-tuple-element.6) | data formatting | bytes 458752

commit v4 on v3

--- a/solution.py
+++ b/solution.py
@@ -12,14 +12,20 @@
 CHIPS = NZ * NY
 BLOCK = 2 * SLOTS
 ROWS = CHIPS * BLOCK
-CHUNKS = 4
-PER = CHIPS // CHUNKS
-CROWS = ROWS // CHUNKS
-HALF = CROWS // 2
+NEAR = NY * BLOCK
+STEPS = (
+    ((0, 1), (2, 3), (4, 5), (6, 7)),
+    ((0,), (1, 2), (3, 4), (5, 6), (7,)),
+)
+CHUNKS = len(STEPS[1])
 F32, BF16 = jnp.float32, jnp.bfloat16
 PARTS = ((0, 768), (768, 1024))
 EXTRA = 128
-FIRST, LAST = (0, 1, 2, 3), (2, 3, 1, 0)
+FIRST, LAST = (0, 1, 2, 3), (3, 4, 2, 1, 0)
+
+
+def span(k, p=1):
+    return STEPS[p][k][0] * NEAR, len(STEPS[p][k]) * NEAR
 
 
 def body(
@@ -27,13 +33,13 @@
     out, amax_in, amax_hid,
     hid_v, gain_v, wg_v, wu_v, wd_v, local_sem, known,
     route, route_sem,
-    ar, af, a_send, a_recv,
+    ar, a_send, a_recv,
     res, sq, sq_send, sq_recv,
     nb, nb_sem, select, combine,
     og, rows, d_send, d_recv, keep_sem,
     g_send, g_recv,
     g_acc, u_acc, act, own, pb, rf, rs, fs, r_send, r_recv,
-    oq, back, b_send, b_recv,
+    oq, back, near, b_send, b_recv, n_send, n_recv,
     mo, mr, m_sem,
     hm, h_send, h_recv, peak,
 ):
@@ -94,28 +100,16 @@
 
     pl.semaphore_wait(barrier, TPS - 1 + 1 + 4)
 
-    h = tokens // 2
-
     def exchange_of(p):
         start, size = PARTS[p]
         at = pl.ds(start, size)
         return [
-            remote(attn.at[0:h, quarter(far, start, size)], af.at[0, :, at], a_send.at[p, 0], a_recv.at[p, 0], me, right),
-            remote(attn.at[h:tokens, quarter(far, start, size)], af.at[1, :, at], a_send.at[p, 1], a_recv.at[p, 1], me, left),
-            remote(attn.at[:, quarter(right, start, size)], ar.at[0, :, at], a_send.at[p, 2], a_recv.at[p, 2], me, right),
-            remote(attn.at[:, quarter(left, start, size)], ar.at[1, :, at], a_send.at[p, 3], a_recv.at[p, 3], me, left),
-            remote(af.at[0, :, at], ar.at[2, 0:h, at], a_send.at[p, 4], a_recv.at[p, 4], me, right),
-            remote(af.at[1, :, at], ar.at[2, h:tokens, at], a_send.at[p, 5], a_recv.at[p, 5], me, left),
+            remote(attn.at[:, quarter(to, start, size)], ar.at[i, :, at], a_send.at[p, i], a_recv.at[p, i], me, to)
+            for i, to in ((2, far), (0, right), (1, left))
         ]
 
     exchange = [exchange_of(p) for p in range(2)]
-
-    def onward(p):
-        for i in range(2):
-            exchange[p][i].wait_recv()
-            exchange[p][4 + i].start()
-
-    for e in exchange[0][:4]:
+    for e in exchange[0]:
         e.start()
     routes = remote(route.at[c], route.at[c], route_sem.at[0], route_sem.at[1], mate, t)
     routes.start()
@@ -123,8 +117,7 @@
         tell(known.at[0], along_z(k), t)
     for k in (1, NY - 1):
         tell(known.at[0], along_y(k), t)
-    onward(0)
-    for e in exchange[1][:4]:
+    for e in exchange[1]:
         e.start()
     pl.semaphore_wait(known.at[0], 4)
     for k in (2, NZ - 2):
@@ -132,14 +125,15 @@
 
     routes.wait_recv()
     both = route[0] + route[1]
-    j = lax.broadcasted_iota(jnp.int32, (ROWS, 128), 0)
-    tok = lax.broadcasted_iota(jnp.int32, (ROWS, 128), 1)
-    d, slot = j >> 3, j & 3
+    j = lax.broadcasted_iota(jnp.int32, (ROWS + NEAR, 128), 0)
+    tok = lax.broadcasted_iota(jnp.int32, (ROWS + NEAR, 128), 1)
+    d, slot = (j >> 3) & (CHIPS - 1), j & 3
+    core = jnp.where(j < ROWS, c, 1 - c)
     m, dy = d >> 2, d & 3
     dz = jnp.where((m & 1) == 1, (m + 1) >> 1, (NZ - (m >> 1)) & (NZ - 1))
-    expert = ((((z + dz) & (NZ - 1)) * NY + ((y + dy) & (NY - 1))) * 2 + c).astype(F32)
-    weight = jnp.zeros((ROWS, 128), F32)
-    match = jnp.zeros((ROWS, 128), F32)
+    expert = ((((z + dz) & (NZ - 1)) * NY + ((y + dy) & (NY - 1))) * 2 + core).astype(F32)
+    weight = jnp.zeros((ROWS + NEAR, 128), F32)
+    match = jnp.zeros((ROWS + NEAR, 128), F32)
     for k in range(8):
         hit = both[k:k + 1, :] == expert
         match = jnp.where(hit, 1.0, match)
@@ -148,10 +142,10 @@
     earlier = jnp.where((a < b) & ((a >> 6) == (b >> 6)), 1.0, 0.0).astype(BF16)
     before = jnp.dot(match.astype(BF16), earlier, preferred_element_type=F32)
     placed = jnp.where((before == slot.astype(F32)) & (((j >> 2) & 1) == (tok >> 6)), match, 0.0)
-    select[...] = placed.astype(BF16)
+    select[...] = placed[0:ROWS].astype(BF16)
     weighted = placed * weight
-    for k in range(CHUNKS):
-        combine[k] = jnp.transpose(weighted[k * CROWS:(k + 1) * CROWS, :]).astype(BF16)
+    for k, (r0, n) in enumerate([span(k) for k in range(CHUNKS)] + [(ROWS, NEAR)]):
+        combine[k, :, 0:n] = jnp.transpose(weighted[r0:r0 + n, :]).astype(BF16)
 
     pl.semaphore_wait(known.at[1], 2)
     for k in range(1, NY):
@@ -163,8 +157,8 @@
 
     def attend(p, squares):
         start, size = PARTS[p]
-        for i in range(2, 6):
-            exchange[p][i].wait_recv()
+        for e in exchange[p]:
+            e.wait_recv()
         for i in range(start // tile, (start + size) // tile):
             s = slice(i * tile, (i + 1) * tile)
             v = hid_v[:, s].astype(F32)
@@ -177,14 +171,14 @@
 
     def swap_of(p):
         start, size = PARTS[p]
-        at = pl.ds(start, size + p * EXTRA)
+        at = pl.ds(start, size)
         return remote(nb.at[here, at], nb.at[here, at], nb_sem.at[p, 0], nb_sem.at[p, 1], mate, t)
 
     def place(m):
         return (m + 1) // 2 if m % 2 else (NZ - m // 2) % NZ
 
-    def hops(k, act_on):
-        for m in (2 * k, 2 * k + 1):
+    def hops(k, act_on, p=1):
+        for m in STEPS[p][k]:
             def one(dy, carry, m=m):
                 act_on(m, dy)
                 return carry
@@ -207,17 +201,18 @@
         start, size = PARTS[p]
         at = slice(start, start + size + p * EXTRA)
         for k in order:
-            r = slice(k * CROWS, (k + 1) * CROWS)
+            r0, n = span(k, p)
+            r = slice(r0, r0 + n)
             og[r, at] = jnp.dot(select[r, :], nb[:, at], preferred_element_type=F32).astype(BF16)
             if k == 0:
                 keep_of(p).start()
-            hops(k, lambda m, dy: outward(p, m, dy).start())
+            hops(k, lambda m, dy: outward(p, m, dy).start(), p)
 
     def gather_of(p, k):
         start, size = PARTS[p]
         at = pl.ds(start, size)
-        r = pl.ds(k * CROWS, CROWS)
-        lo, hi = pl.ds(k * CROWS, HALF), pl.ds(k * CROWS + HALF, HALF)
+        r0, n = span(k, p)
+        r, lo, hi = pl.ds(r0, n), pl.ds(r0, n // 2), pl.ds(r0 + n // 2, n // 2)
         snd, rcv = [g_send.at[p, k, i] for i in range(4)], [g_recv.at[p, k, i] for i in range(4)]
         return [
             remote(rows.at[0, r, at], rows.at[1, r, at], snd[0], rcv[0], me, right),
@@ -226,12 +221,12 @@
             remote(rows.at[3, hi, at], rows.at[2, hi, at], snd[3], rcv[3], me, left),
         ]
 
-    gathers = [[gather_of(p, k) for k in range(CHUNKS)] for p in range(2)]
+    gathers = [[gather_of(p, k) for k in range(len(STEPS[p]))] for p in range(2)]
 
     def fetch(p, k):
         if k == 0:
             keep_of(p).wait()
-        hops(k, lambda m, dy: outward(p, m, dy).wait_recv())
+        hops(k, lambda m, dy: outward(p, m, dy).wait_recv(), p)
         gathers[p][k][0].start()
         gathers[p][k][1].start()
 
@@ -246,10 +241,11 @@
 
     def hidden_rows(p, k):
         start, size = PARTS[p]
-        r = slice(k * CROWS, (k + 1) * CROWS)
+        r0, n = span(k, p)
+        r = slice(r0, r0 + n)
         if p == 0:
-            g = jnp.zeros((CROWS, wg_v.shape[1]), F32)
-            u = jnp.zeros((CROWS, wu_v.shape[1]), F32)
+            g = jnp.zeros((n, wg_v.shape[1]), F32)
+            u = jnp.zeros((n, wu_v.shape[1]), F32)
         else:
             g, u = g_acc[r, :], u_acc[r, :]
         for q, src in ((0, t), (1, left), (2, far), (3, right)):
@@ -266,19 +262,19 @@
             v = (g / (1.0 + jnp.exp(-g)) * u).astype(BF16)
             act[r, :] = v
             v = jnp.abs(v.astype(F32))
-            peak[...] = jnp.maximum(peak[...], jnp.max(v.reshape(CROWS // 8, 8, v.shape[1]), axis=0))
+            peak[...] = jnp.maximum(peak[...], jnp.max(v.reshape(n // 8, 8, v.shape[1]), axis=0))
 
     def down(k):
-        r = slice(k * CROWS, (k + 1) * CROWS)
+        r0, n = span(k)
+        r = slice(r0, r0 + n)
         x = act[r, :]
         for i, dst in ((1, far), (0, right), (2, left)):
             pb[i, r, :] = jnp.dot(x, wd_v[:, quarter(dst)], preferred_element_type=F32).astype(BF16)
         own[r, :] = jnp.dot(x, wd_v[:, quarter(t)], preferred_element_type=F32)
 
     def reduce_of(k):
-        r0 = k * CROWS
-        lo, hi = pl.ds(r0, HALF), pl.ds(r0 + HALF, HALF)
-        f = pl.ds(k * HALF, HALF)
+        r0, n = span(k)
+        lo, hi, f = pl.ds(r0, n // 2), pl.ds(r0 + n // 2, n // 2), pl.ds(r0 // 2, n // 2)
         snd, rcv = [r_send.at[k, i] for i in range(6)], [r_recv.at[k, i] for i in range(6)]
         return [
             remote(pb.at[1, lo], rf.at[0, f], snd[0], rcv[0], me, right),
@@ -301,13 +297,13 @@
                 reduces[k][i].start()
 
     def second_hop(k):
-        r0 = k * CROWS
-        f = slice(k * HALF, (k + 1) * HALF)
+        r0, n = span(k)
+        f = slice(r0 // 2, (r0 + n) // 2)
         reduces[k][0].wait_recv()
-        fs[0, f] = (rf[0, f].astype(F32) + pb[0, r0:r0 + HALF].astype(F32)).astype(BF16)
+        fs[0, f] = (rf[0, f].astype(F32) + pb[0, r0:r0 + n // 2].astype(F32)).astype(BF16)
         reduces[k][4].start()
         reduces[k][1].wait_recv()
-        fs[1, f] = (rf[1, f].astype(F32) + pb[2, r0 + HALF:r0 + CROWS].astype(F32)).astype(BF16)
+        fs[1, f] = (rf[1, f].astype(F32) + pb[2, r0 + n // 2:r0 + n].astype(F32)).astype(BF16)
         reduces[k][5].start()
 
     def homeward(m, dy):
@@ -317,25 +313,39 @@
 
     stay = pltpu.make_async_copy(oq.at[0:BLOCK], back.at[0:BLOCK], keep_sem.at[2])
 
+    def across(dy):
+        dp = (z * NY + lax.rem(y + NY - dy, NY)) * 2 + 1 - c
+        return remote(oq.at[block(dy)], near.at[block(dy)], n_send.at[dy], n_recv.at[dy], dp, t)
+
     def send_back(k):
-        r = slice(k * CROWS, (k + 1) * CROWS)
+        r0, n = span(k)
+        r = slice(r0, r0 + n)
         for i in range(2, 6):
             reduces[k][i].wait_recv()
         oq[r, :] = (own[r, :] + rs[0, r].astype(F32) + rs[1, r].astype(F32)).astype(BF16)
         if k == 0:
+            for dy in range(NY):
+                across(dy).start()
             stay.start()
         hops(k, lambda m, dy: homeward(m, dy).start())
 
     def collect(k):
-        r = slice(k * CROWS, (k + 1) * CROWS)
-        if k == 0:
-            stay.wait()
+        r0, n = span(k)
+        r = slice(r0, r0 + n)
         hops(k, lambda m, dy: homeward(m, dy).wait_recv())
-        got = jnp.dot(combine[k, there, :], back[r, :], preferred_element_type=F32)
-        mo[...] = got if k == LAST[0] else mo[...] + got
-        if k == LAST[-1]:
-            give.start()
-        res[...] = res[...] + jnp.dot(combine[k, here, :], back[r, :], preferred_element_type=F32)
+        if k:
+            got = jnp.dot(combine[k, there, 0:n], back[r, :], preferred_element_type=F32)
+            mo[...] = got if k == LAST[0] else mo[...] + got
+            if k == LAST[-2]:
+                give.start()
+            res[...] = res[...] + jnp.dot(combine[k, here, 0:n], back[r, :], preferred_element_type=F32)
+            return
+        stay.wait()
+        for dy in range(NY):
+            across(dy).wait_recv()
+        last = jnp.dot(combine[0, here, 0:n], back[r, :], preferred_element_type=F32)
+        last = last + jnp.dot(combine[CHUNKS, here, 0:n], near[...], preferred_element_type=F32)
+        out[...] = (res[...] + last).astype(BF16)
 
     give = remote(mo, mr, m_sem.at[0], m_sem.at[1], mate, t)
 
@@ -344,45 +354,54 @@
     squares = attend(0, jnp.zeros((tokens, tile), F32))
     swaps = [swap_of(p) for p in range(2)]
     swaps[0].start()
-    onward(1)
     pl.semaphore_wait(known.at[2], NY - 1)
     swaps[0].wait_recv()
     dispatch(0, FIRST)
+    units = [(0, k) for k in FIRST] + [(1, k) for k in LAST]
     squares = attend(1, squares)
-    sq[0] = jnp.broadcast_to(jnp.sum(squares, axis=1, keepdims=True), (tokens, 128))
+    swaps[1].start()
+    total = jnp.sum(squares, axis=1, keepdims=True)
+    total = jnp.transpose(jnp.broadcast_to(total, (tokens, 128)))[0:8, :]
+    sq[0] = jnp.where(mine, jnp.concatenate([total, total], axis=1), 0.0)
     share = [
-        remote(sq.at[0], sq.at[r], sq_send.at[r - 1], sq_recv.at[r - 1], me, lax.rem(t + r, TPS))
-        for r in range(1, TPS)
+        remote(sq.at[0], sq.at[2 * r + x], sq_send.at[2 * r + x], sq_recv.at[2 * r + x],
+               mate if x else me, lax.rem(t + r, TPS))
+        for r in range(TPS) for x in range(2) if r or x
     ]
     for s in share:
         s.start()
-    fetch(0, FIRST[0])
+    fetch(*units[0])
     for s in share:
         s.wait_recv()
-    inv = lax.rsqrt((sq[0] + sq[1] + sq[2] + sq[3]) / width + EPS)
+    total = sq[0]
+    for i in range(1, 2 * TPS):
+        total = total + sq[i]
+    inv = lax.rsqrt(total[0:1, :] / width + EPS)
     high = inv.astype(BF16).astype(F32)
     middle = (inv - high).astype(BF16).astype(F32)
-    at = lax.broadcasted_iota(jnp.int32, (tokens, EXTRA), 1)
+    at = lax.broadcasted_iota(jnp.int32, (EXTRA, 128), 0)
     terms = jnp.where(at == 0, high, jnp.where(at == 1, middle, jnp.where(at == 2, inv - high - middle, 0.0)))
-    nb[here, cols:cols + EXTRA] = terms.astype(BF16)
-    swaps[1].start()
-    fetch(0, FIRST[1])
-    pass_on(0, FIRST[0])
+    nb[:, cols:cols + EXTRA] = jnp.transpose(terms).astype(BF16)
     swaps[1].wait_recv()
-    dispatch(1, LAST)
+    dispatch(1, LAST[:2])
+    fetch(*units[1])
+    pass_on(*units[0])
+    dispatch(1, LAST[2:])
+    fetch(*units[2])
+    pass_on(*units[1])
     peak[...] = jnp.zeros(peak.shape, F32)
 
-    units = [(0, k) for k in FIRST] + [(1, k) for k in LAST]
     n = len(units)
-    for i in range(2, n + 4):
+    for i in range(3, n + 4):
         if i < n:
             fetch(*units[i])
         if i - 1 < n:
             pass_on(*units[i - 1])
-        if i == 2:
+        if i == 3:
             for load in loads[3:]:
                 load.wait()
-        if i - 3 >= CHUNKS and i - 3 < n:
+            finish(*units[0])
+        if i - 3 >= len(FIRST) and i - 3 < n:
             second_hop(units[i - 3][1])
         if i - 2 < n:
             finish(*units[i - 2])
@@ -394,40 +413,48 @@
             ]
             for s in tops:
                 s.start()
-        if i == n + 1:
-            largest = jnp.zeros((CROWS, 1), F32)
-            for k in range(CHUNKS):
-                r = slice(k * CROWS, (k + 1) * CROWS)
-                top = jnp.zeros((CROWS, 128), F32)
+        if i - 4 >= len(FIRST):
+            send_back(units[i - 4][1])
+        if i == n + 2:
+            largest = jnp.zeros((NEAR, 1), F32)
+            for k in range(ROWS // NEAR):
+                r = slice(k * NEAR, (k + 1) * NEAR)
+                top = jnp.zeros((NEAR, 128), F32)
                 for q in range(4):
                     for l in range(cols // 128):
                         top = jnp.maximum(top, jnp.abs(rows[q, r, l * 128:(l + 1) * 128].astype(F32)))
                 largest = jnp.maximum(largest, jnp.max(top, axis=1, keepdims=True) * factor(r))
             amax_in[0] = jnp.max(largest)
-        if i - 4 >= CHUNKS:
-            send_back(units[i - 4][1])
-        if i == n + 2:
             for s in tops:
                 s.wait_recv()
             amax_hid[0] = jnp.max(jnp.maximum(jnp.maximum(hm[0], hm[1]), jnp.maximum(hm[2], hm[3])))
+            for s in (*exchange[0], *exchange[1], routes, *share, *swaps):
+                s.wait_send()
+            for g in (*gathers[0], *gathers[1], *(reduces[k] for k in LAST[:-2])):
+                for s in g:
+                    s.wait_send()
+
+            def drain(m, dy):
+                outward(0, m, dy).wait_send()
+                outward(1, m, dy).wait_send()
+
+            for k in range(CHUNKS):
+                hops(k, drain)
             collect(LAST[0])
-    for k in LAST[1:]:
+            for k in LAST[:-2]:
+                hops(k, lambda m, dy: homeward(m, dy).wait_send())
+    for k in LAST[1:-1]:
         collect(k)
     give.wait_recv()
-    out[...] = (res[...] + mr[...]).astype(BF16)
-
-    for s in (*exchange[0], *exchange[1], routes, *share, *swaps, *tops, give):
+    res[...] = res[...] + mr[...]
+    collect(LAST[-1])
+
+    for s in (*tops, give, *reduces[LAST[-2]], *reduces[LAST[-1]]):
         s.wait_send()
-    for k in range(CHUNKS):
-        for s in (*gathers[0][k], *gathers[1][k], *reduces[k]):
-            s.wait_send()
-
-        def drain(m, dy):
-            outward(0, m, dy).wait_send()
-            outward(1, m, dy).wait_send()
-            homeward(m, dy).wait_send()
-
-        hops(k, drain)
+    for k in LAST[-2:]:
+        hops(k, lambda m, dy: homeward(m, dy).wait_send())
+    for dy in range(NY):
+        across(dy).wait_send()
 
 
 def on_device(attn_partial, hidden_in, norm_gain, expert_ids, route_prob, w_gate, w_up, w_down):
@@ -441,15 +468,15 @@
         V((tokens, cols), BF16), V((1, cols), F32), V((width, ff), BF16), V((width, ff), BF16), V((ff, width), BF16), dma((6,)),
         pltpu.SemaphoreType.REGULAR((3,)),
         V((2, 16, 128), F32), dma((2,)),
-        V((4, tokens, cols), BF16), V((2, tokens // 2, cols), BF16), dma((2, 6)), dma((2, 6)),
-        V((tokens, cols), F32), V((4, tokens, 128), F32), dma((3,)), dma((3,)),
-        V((2 * tokens, cols + EXTRA), BF16), dma((2, 2)), V((ROWS, 128), BF16), V((CHUNKS, 128, CROWS), BF16),
+        V((4, tokens, cols), BF16), dma((2, 3)), dma((2, 3)),
+        V((tokens, cols), F32), V((2 * TPS, 8, 128), F32), dma((2 * TPS,)), dma((2 * TPS,)),
+        V((2 * tokens, cols + EXTRA), BF16), dma((2, 2)), V((ROWS, 128), BF16), V((CHUNKS + 1, 128, 128), BF16),
         V((ROWS, cols + EXTRA), BF16), V((4, ROWS, cols + EXTRA), BF16), dma((2, CHIPS)), dma((2, CHIPS)), dma((3,)),
         dma((2, CHUNKS, 4)), dma((2, CHUNKS, 4)),
         V((ROWS, ff), F32), V((ROWS, ff), F32),
         V((ROWS, ff), BF16), V((ROWS, cols), F32), V((3, ROWS, cols), BF16), V((2, ROWS // 2, cols), BF16),
         V((2, ROWS, cols), BF16), V((2, ROWS // 2, cols), BF16), dma((CHUNKS, 6)), dma((CHUNKS, 6)),
-        V((ROWS, cols), BF16), V((ROWS, cols), BF16), dma((CHIPS,)), dma((CHIPS,)),
+        V((ROWS, cols), BF16), V((ROWS, cols), BF16), V((NEAR, cols), BF16), dma((CHIPS,)), dma((CHIPS,)), dma((NY,)), dma((NY,)),
         V((tokens, cols), F32), V((tokens, cols), F32), dma((2,)),
         V((4, 8, 128), F32), dma((3,)), dma((3,)), V((8, 256), F32),
     ]

time: 110 us -> 108 us (0.982)
  Pallas kernels: 104 us -> 102 us
    pallas_call x1, Pallas kernels: 104 us -> 102 us  [on_device(): pl.pallas_call(body, out_shape=(jax.ShapeDtypeStruct((tokens, cols), BF16...]
where the time goes in v4:
time: 108 us; the launch traced here: 107 us
  Pallas kernels  102 us (94%)
  between operations  4.15 us (4%)
  local copies, waits for them, and re-layouts  1.64 us (2%)
    pallas_call x1, Pallas kernels, on_device(): pl.pallas_call(body, out_shape=(jax.ShapeDtypeStruct((tokens, cols), BF16...  102 us

profile of v4, /device:TPU:1, one launch (start us, length us, event | category | flops | bytes accessed | tf_op | source)
XLA Modules:
  0.0 107.5 jit_solution(10481388150090279698)
XLA Ops:
  0.6 101.7 %shard_map.103 = (bf16[64,1792]{1,0:T(8,128)(2,1)}, f32[1]{0:T(128)}, f32[1]{0:T(128)}) custom-call(s32[8,64]{1,0:T(8,128)} %bitcast.12, bf16[8,64]{1,0:T(8,128)(2,1)} %bitcast.13, bf16[64,7168]{1,0:T(8,128)(2,1)} %bitcast.10, bf16[64,1792]{1,0:T(8,128)(2,1)} %hidden.1, f32[1,7168]{1,0:T(1,128)} %bitcast.11, bf16[7168,256]{1,0:T(8,128)(2,1)} %bitcast.7, ...), custom_call_target="tpu_custom_call" | custom-call | tf_op jit(solution)/shard_map/pallas_call | solution.py:483
  102.3 1.6 %copy.14 = bf16[64,1792]{1,0:T(8,128)(2,1)} copy(bf16[64,1792]{1,0:T(8,128)(2,1)} %get-tuple-element.6) | data formatting | bytes 458752
